TPU v7x, 32 devices: a whole 2x2x4 slice. The times are simulated.
32 devices in a mesh: dp: 4 (over y, x), replica: 8 (over z, core).
Axes of the slice: x: 2, y: 2, z: 4, core: 2. Of those that a mesh axis runs over, the one named last changes fastest.
Arguments:
- events: bfloat16 [8192, 512], P(('dp', 'replica')), may hold values from -6 to 6
- cotangent: bfloat16 [8192, 512], P(('dp', 'replica')), may hold values from -6 to 6
- weight_in: bfloat16 [512, 2048], replicated, may hold values from -0.25 to 0.25
- weight_out: bfloat16 [512, 512], replicated, may hold values from -0.25 to 0.25
- plan_dest: int32 [8192], P(('dp', 'replica')), may hold values from 0 to 3, as said below
- plan_pos: int32 [8192], P(('dp', 'replica')), may hold values from 0 to 255, as said below
- seq_lengths: int32 [32, 8], P(('dp', 'replica')), may hold values from 1 to 128, 256 in all within a row
Outputs:
- grad_events: bfloat16 [8192, 512], P(('dp', 'replica'))
- grad_weight_in: float32 [512, 2048], P(None, 'dp')
- grad_weight_out: float32 [512, 512], P('dp')
Inputs may be any that keep to these rules, and one draw needn't show every extreme that they name: `plan_dest`: rows stay within their replica's group. From one loader to one compute device go at most 96 rows, and exactly 96 for some pairs of every group; every compute device receives 256 rows. `plan_pos`: the rows that one compute device receives take each position 0 to 255 once. `seq_lengths`: each row sums to 256.
All inputs are finite; a program needn't handle non-finite values.
Results may differ from a plain program's by a relative error of at most 0.014.
Values may be sent and summed in bfloat16 or wider, within the bound.
A program may use at most 64 MiB of HBM per device.

v0:
```python
import functools

import jax
import jax.numpy as jnp
from jax import lax
from jax.experimental import pallas as pl
from jax.experimental.pallas import tpu as pltpu
from jax.sharding import PartitionSpec as P

HEADS = 8
MAXLEN = 128
COLORS = 1
EPS = 1e-05
LANES = 128
MESH = pl.DeviceIdType.MESH
F32 = jnp.float32
BF16 = jnp.bfloat16


def contract(left, right, dims):
    return lax.dot_general(left, right, ((dims[:1], dims[1:]), ((), ())), preferred_element_type=F32)


def nn(left, right):
    return contract(left, right, (1, 0))


def nt(left, right):
    return contract(left, right, (1, 1))


def tn(left, right):
    return contract(left, right, (0, 0))


def normalize(values):
    center = values - jnp.mean(values, axis=-1, keepdims=True)
    inverse = lax.rsqrt(jnp.mean(center * center, axis=-1, keepdims=True) + EPS)
    return center * inverse, inverse


def norm_back(grad, normed, inverse):
    return inverse * (
        grad
        - jnp.mean(grad, axis=-1, keepdims=True)
        - normed * jnp.mean(grad * normed, axis=-1, keepdims=True)
    )


def prep_kernel(slot_count, dest_ref, pos_ref, ev_ref, ct_ref, send_ref, pick_ref):
    rows, width = ev_ref.shape
    group = send_ref.shape[0]
    dest = dest_ref[...]
    hot = lax.broadcasted_iota(jnp.int32, (8, rows), 0) == dest
    upper = lax.broadcasted_iota(jnp.int32, (rows, rows), 0) < lax.broadcasted_iota(
        jnp.int32, (rows, rows), 1
    )
    earlier = nn(
        jnp.where(hot, 1.0, 0.0).astype(BF16), jnp.where(upper, 1.0, 0.0).astype(BF16)
    )
    slot = jnp.sum(jnp.where(hot, earlier, 0.0), axis=0, keepdims=True).astype(jnp.int32)
    flat = dest * slot_count + slot
    total = group * slot_count
    chosen = lax.broadcasted_iota(jnp.int32, (total, rows), 0) == flat
    pick = jnp.where(chosen, 1.0, 0.0).astype(BF16)
    pick_ref[...] = pick
    place = jnp.sum(
        jnp.where(chosen, pos_ref[...].astype(F32) + 1.0, 0.0), axis=1, keepdims=True
    )
    shape = (group, slot_count)
    send_ref[:, :, :width] = nn(pick, ev_ref[...]).astype(BF16).reshape(shape + (width,))
    send_ref[:, :, width : 2 * width] = nn(pick, ct_ref[...]).astype(BF16).reshape(shape + (width,))
    send_ref[:, :, 2 * width :] = (
        jnp.broadcast_to(place, (total, LANES)).astype(BF16).reshape(shape + (LANES,))
    )


def swap_kernel(send_ref, recv_ref, send_sem, recv_sem, own_sem):
    group = lax.axis_size("dp")
    me = lax.axis_index("dp")
    barrier = pltpu.get_barrier_semaphore()
    for step in range(1, group):
        pl.semaphore_signal(
            barrier, inc=1, device_id={"dp": lax.rem(me + step, group)}, device_id_type=MESH
        )
    own = pltpu.make_async_copy(send_ref.at[me], recv_ref.at[me], own_sem)
    own.start()
    pl.semaphore_wait(barrier, group - 1)
    copies = []
    for step in range(1, group):
        peer = lax.rem(me + step, group)
        copy = pltpu.make_async_remote_copy(
            src_ref=send_ref.at[peer],
            dst_ref=recv_ref.at[me],
            send_sem=send_sem.at[step],
            recv_sem=recv_sem.at[step],
            device_id={"dp": peer},
            device_id_type=MESH,
        )
        copy.start()
        copies.append(copy)
    own.wait()
    for copy in copies:
        copy.wait()


def layer_kernel(
    len_ref,
    recv_ref,
    win_ref,
    wout_ref,
    out_ref,
    *rest,
):
    xn_out, gproj, gated_out, g_out, act, slope_p, attn, slope_s = rest
    group, slots, packed = recv_ref.shape
    width = wout_ref.shape[0]
    rows = act.shape[0]
    head = width // HEADS
    scale = 1.0 / head**0.5
    total = group * slots
    got = recv_ref[...].reshape(total, packed)
    place = got[:, 2 * width : 2 * width + 1].astype(F32) - 1.0
    spots = lax.broadcasted_iota(jnp.int32, (total, rows), 1).astype(F32)
    pick = jnp.where(place == spots, 1.0, 0.0).astype(BF16)
    tokens = tn(pick, got[:, :width])
    grad = tn(pick, got[:, width : 2 * width])
    grad16 = grad.astype(BF16)
    normed, inverse = normalize(tokens)
    xn = normed.astype(BF16)
    for block in range(4):
        cols = slice(block * width, (block + 1) * width)
        proj = nn(xn, win_ref[:, cols])
        sig = jax.nn.sigmoid(proj)
        act[:, cols] = (proj * sig).astype(BF16)
        slope_p[:, cols] = sig * (1.0 + proj * (1.0 - sig))
    row_at = lax.broadcasted_iota(jnp.int32, (rows, 1), 0)
    col_at = lax.broadcasted_iota(jnp.int32, (1, rows), 1)
    bound = jnp.int32(0)
    row_seg = jnp.zeros((rows, 1), jnp.int32)
    col_seg = jnp.zeros((1, rows), jnp.int32)
    for seq in range(len_ref.shape[1]):
        bound = bound + len_ref[0, seq]
        row_seg = row_seg + jnp.where(row_at >= bound, 1, 0)
        col_seg = col_seg + jnp.where(col_at >= bound, 1, 0)
    mask = (row_seg == col_seg) & (col_at <= row_at)
    pair = 2 * head
    low = lax.broadcasted_iota(jnp.int32, (rows, pair), 1) < head

    def half(values, which):
        return jnp.where(low if which == 0 else ~low, values, jnp.zeros_like(values))

    def cut(block, duo):
        start = block * width + duo * pair
        return act[:, start : start + pair]

    outs = []
    for duo in range(HEADS // 2):
        value, query, key = cut(1, duo), cut(2, duo), cut(3, duo)
        parts = []
        for which in range(2):
            at = 2 * duo + which
            scores = nt(half(query, which), key) * scale
            sig = jax.nn.sigmoid(scores)
            weight = jnp.where(mask, scores * sig * (1.0 / MAXLEN), 0.0).astype(BF16)
            attn[at] = weight
            slope_s[at] = jnp.where(
                mask, sig * (1.0 + scores * (1.0 - sig)) * (scale / MAXLEN), 0.0
            )
            parts.append(nn(weight, value))
        outs.append(jnp.where(low, parts[0], parts[1]))
    onorm, oinv = normalize(jnp.concatenate(outs, axis=1))
    gate = act[:, :width].astype(F32)
    gated = (gate * onorm).astype(BF16)
    grad_z = nt(grad16, wout_ref[...])
    gproj[:, :width] = (grad_z * onorm * slope_p[:, :width]).astype(BF16)
    grad_out = norm_back(grad_z * gate, onorm, oinv).astype(BF16)
    for duo in range(HEADS // 2):
        value, query, key = cut(1, duo), cut(2, duo), cut(3, duo)
        gout = grad_out[:, duo * pair : (duo + 1) * pair]
        parts = ([], [], [])
        for which in range(2):
            at = 2 * duo + which
            gscore = (nt(half(gout, which), value) * slope_s[at]).astype(BF16)
            parts[0].append(tn(attn[at], gout))
            parts[1].append(nn(gscore, key))
            parts[2].append(tn(gscore, query))
        for block in range(3):
            start = (block + 1) * width + duo * pair
            cols = slice(start, start + pair)
            both = jnp.where(low, parts[block][0], parts[block][1])
            gproj[:, cols] = (both * slope_p[:, cols]).astype(BF16)
    grad_xn = nt(gproj[...], win_ref[...])
    grad_tokens = (grad + norm_back(grad_xn, normed, inverse)).astype(BF16)
    out_ref[...] = nn(pick, grad_tokens).astype(BF16).reshape(group, slots, width)
    xn_out[...] = xn
    gated_out[...] = gated
    g_out[...] = grad16


def whole_kernel(
    slots,
    len_ref,
    dest_ref,
    pos_ref,
    ev_ref,
    ct_ref,
    win_any,
    wout_any,
    grad_ref,
    final_ref,
    win_ref,
    wout_ref,
    pick_ref,
    back_ref,
    ev_send,
    ct_send,
    at_send,
    ev_got,
    ct_got,
    at_got,
    act,
    slope_p,
    gproj,
    attn,
    slope_s,
    xn_ref,
    out_ref,
    b_ref,
    give_ref,
    keep_ref,
    core_got,
    one_send,
    one_got,
    two_keep,
    two_send,
    two_got,
    dp_sum,
    z_got,
    own_sems,
    win_sem,
    wout_sem,
    row_send,
    row_recv,
    core_send,
    core_recv,
    one_ssem,
    one_rsem,
    two_ssem,
    two_rsem,
    z_send,
    z_recv,
    all_send,
    all_recv,
    fwd_send,
    fwd_recv,
):
    rows, width = ev_ref.shape
    group = ev_send.shape[0]
    chain = keep_ref.shape[0]
    total = group * slots
    head = width // HEADS
    scale = 1.0 / head**0.5
    me = lax.axis_index("dp")
    rep = lax.axis_index("replica")
    core = lax.rem(rep, 2)
    other = 1 - core
    spot = rep // 2
    partner = {"replica": spot * 2 + other}
    low_bit, high_bit = lax.rem(me, 2), me // 2
    near = high_bit * 2 + 1 - low_bit
    far = (1 - high_bit) * 2 + low_bit
    first = other * near + core * far
    second = core * near + other * far
    third = 3 - me

    def dp_peer(step):
        return lax.rem(me + step, group)

    def z_peer(step):
        return lax.rem(spot + step, chain)

    def z_id(step):
        return {"replica": z_peer(step) * 2 + core}

    win_copy = pltpu.make_async_copy(win_any, win_ref, win_sem)
    wout_copy = pltpu.make_async_copy(wout_any, wout_ref, wout_sem)
    barrier = pltpu.get_barrier_semaphore()
    for step in range(1, group):
        pl.semaphore_signal(barrier, inc=1, device_id={"dp": dp_peer(step)}, device_id_type=MESH)
    pl.semaphore_signal(barrier, inc=1, device_id=partner, device_id_type=MESH)
    for step in range(1, chain):
        pl.semaphore_signal(barrier, inc=1, device_id=z_id(step), device_id_type=MESH)

    def send(src, dst, sems, at, device):
        copy = pltpu.make_async_remote_copy(
            src_ref=src,
            dst_ref=dst,
            send_sem=sems[0].at[at],
            recv_sem=sems[1].at[at],
            device_id=device,
            device_id_type=MESH,
        )
        copy.start()
        return copy

    dest = dest_ref[...]
    hot = lax.broadcasted_iota(jnp.int32, (8, rows), 0) == dest
    upper = lax.broadcasted_iota(jnp.int32, (rows, rows), 0) < lax.broadcasted_iota(
        jnp.int32, (rows, rows), 1
    )
    earlier = nn(
        jnp.where(hot, 1.0, 0.0).astype(BF16), jnp.where(upper, 1.0, 0.0).astype(BF16)
    )
    slot = jnp.sum(jnp.where(hot, earlier, 0.0), axis=0, keepdims=True).astype(jnp.int32)
    slot_iota = lax.broadcasted_iota(jnp.int32, (total, rows), 0)
    pick = jnp.where(slot_iota == dest * slots + slot, 1.0, 0.0).astype(BF16)
    pick_ref[...] = pick
    packed = (group, slots, width)
    ev_send[...] = nn(pick, ev_ref[...]).astype(BF16).reshape(packed)
    win_copy.start()
    wout_copy.start()
    pl.semaphore_wait(barrier, group + chain - 1)
    row_copies = ([], [], [])
    own_copies = []

    def rows_out(kind, src, dst):
        for step in range(1, group):
            peer = dp_peer(step)
            row_copies[kind].append(
                send(
                    src.at[peer],
                    dst.at[me],
                    (row_send, row_recv),
                    kind * group + step,
                    {"dp": peer},
                )
            )
        own = pltpu.make_async_copy(src.at[me], dst.at[me], own_sems.at[kind])
        own.start()
        own_copies.append(own)

    rows_out(0, ev_send, ev_got)
    spots = jnp.broadcast_to(pos_ref[...] + 1, (8, rows)).astype(F32).astype(BF16)
    landing = slot_iota == me * slots + slot
    for dp in range(group):
        there = jnp.where(landing & (dest == dp), 1.0, 0.0).astype(BF16)
        at_send[dp] = nt(spots, there)
    rows_out(1, at_send, at_got)
    ct_send[...] = nn(pick, ct_ref[...]).astype(BF16).reshape(packed)
    rows_out(2, ct_send, ct_got)

    for kind in range(2):
        own_copies[kind].wait()
        for copy in row_copies[kind]:
            copy.wait_recv()
    place = at_got[0]
    for dp in range(1, group):
        place = place + at_got[dp]
    row_iota = lax.broadcasted_iota(jnp.int32, (rows, total), 0).astype(F32) + 1.0
    fetch = jnp.where(row_iota == place[:1], 1.0, 0.0).astype(BF16)
    tokens = nn(fetch, ev_got[...].reshape(total, width))
    normed, inverse = normalize(tokens)
    xn = normed.astype(BF16)
    xn_ref[...] = xn
    win_copy.wait()
    wout_copy.wait()
    for block in range(4):
        cols = slice(block * width, (block + 1) * width)
        proj = nn(xn, win_ref[:, cols])
        sig = jax.nn.sigmoid(proj)
        act[:, cols] = (proj * sig).astype(BF16)
        slope_p[:, cols] = sig * (1.0 + proj * (1.0 - sig))
    row_at = lax.broadcasted_iota(jnp.int32, (rows, 1), 0)
    col_at = lax.broadcasted_iota(jnp.int32, (1, rows), 1)
    bound = jnp.int32(0)
    row_seg = jnp.zeros((rows, 1), jnp.int32)
    col_seg = jnp.zeros((1, rows), jnp.int32)
    for seq in range(len_ref.shape[1]):
        bound = bound + len_ref[0, seq]
        row_seg = row_seg + jnp.where(row_at >= bound, 1, 0)
        col_seg = col_seg + jnp.where(col_at >= bound, 1, 0)
    mask = (row_seg == col_seg) & (col_at <= row_at)
    pair = 2 * head
    low = lax.broadcasted_iota(jnp.int32, (rows, pair), 1) < head

    def half(values, which):
        return jnp.where(low if which == 0 else ~low, values, jnp.zeros_like(values))

    def cut(block, duo):
        start = block * width + duo * pair
        return act[:, start : start + pair]

    outs = []
    for duo in range(HEADS // 2):
        value, query, key = cut(1, duo), cut(2, duo), cut(3, duo)
        parts = []
        for which in range(2):
            at = 2 * duo + which
            scores = nt(half(query, which), key) * scale
            sig = jax.nn.sigmoid(scores)
            weight = jnp.where(mask, scores * sig * (1.0 / MAXLEN), 0.0).astype(BF16)
            attn[at] = weight
            slope_s[at] = jnp.where(
                mask, sig * (1.0 + scores * (1.0 - sig)) * (scale / MAXLEN), 0.0
            )
            parts.append(nn(weight, value))
        outs.append(jnp.where(low, parts[0], parts[1]))
    onorm, oinv = normalize(jnp.concatenate(outs, axis=1))
    gate = act[:, :width].astype(F32)
    gated = (gate * onorm).astype(BF16)

    own_copies[2].wait()
    for copy in row_copies[2]:
        copy.wait_recv()
    grad = nn(fetch, ct_got[...].reshape(total, width))
    grad16 = grad.astype(BF16)
    grad_z = nt(grad16, wout_ref[...])
    gproj[:, :width] = (grad_z * onorm * slope_p[:, :width]).astype(BF16)
    share_in = width // (2 * chain)
    share_out = width // (group * 2 * chain)
    whole_out = tn(gated, grad16).astype(BF16).reshape(group, 2, chain, share_out, width)
    for dp in range(group):
        b_ref[:, :, dp] = whole_out[dp]
    grad_out = norm_back(grad_z * gate, onorm, oinv).astype(BF16)
    for duo in range(HEADS // 2):
        value, query, key = cut(1, duo), cut(2, duo), cut(3, duo)
        gout = grad_out[:, duo * pair : (duo + 1) * pair]
        parts = ([], [], [])
        for which in range(2):
            at = 2 * duo + which
            gscore = (nt(half(gout, which), value) * slope_s[at]).astype(BF16)
            parts[0].append(tn(attn[at], gout))
            parts[1].append(nn(gscore, key))
            parts[2].append(tn(gscore, query))
        for block in range(3):
            start = (block + 1) * width + duo * pair
            cols = slice(start, start + pair)
            both = jnp.where(low, parts[block][0], parts[block][1])
            gproj[:, cols] = (both * slope_p[:, cols]).astype(BF16)

    wave = width // COLORS

    def lanes(color):
        return slice(color * wave, (color + 1) * wave)

    def partials(which, into, color):
        across = width // 2
        columns = pl.ds(pl.multiple_of(which * across, across), across)
        left = xn_ref[:, columns]
        for dp in range(group):
            start = dp * width + color * wave
            shard = tn(left, gproj[:, start : start + wave]).astype(BF16)
            into[:, dp, :share_in, lanes(color)] = shard.reshape(chain, share_in, wave)
        into[:, :, share_in:, lanes(color)] = b_ref[which, :, :, :, lanes(color)]

    core_copies, one_copies, two_copies, z_copies = [], [], [], []
    for color in range(COLORS):
        partials(other, give_ref, color)
        for hop in range(1, chain + 1):
            step = color * chain + hop - 1
            core_copies.append(
                send(
                    give_ref.at[z_peer(hop), :, :, lanes(color)],
                    core_got.at[step],
                    (core_send, core_recv),
                    step,
                    partner,
                )
            )

    def stage_one(step):
        at = z_peer(step % chain + 1)
        cols = lanes(step // chain)
        core_copies[step].wait_recv()

        def both(dp):
            return keep_ref[at, dp, :, cols].astype(F32) + core_got[step, dp].astype(F32)

        one_send[step, 0] = both(first).astype(BF16)
        one_send[step, 1] = both(third).astype(BF16)
        one_copies.append(
            send(one_send.at[step], one_got.at[step], (one_ssem, one_rsem), step, {"dp": first})
        )
        two_keep[step, 0] = both(me)
        two_keep[step, 1] = both(second)

    def stage_two(step):
        one_copies[step].wait_recv()
        two_send[step] = (two_keep[step, 1] + one_got[step, 1].astype(F32)).astype(BF16)
        two_copies.append(
            send(two_send.at[step], two_got.at[step], (two_ssem, two_rsem), step, {"dp": second})
        )

    def stage_three(step):
        two_copies[step].wait_recv()
        dp_sum[step] = (
            two_keep[step, 0] + one_got[step, 0].astype(F32) + two_got[step].astype(F32)
        ).astype(BF16)
        hop = step % chain + 1
        if hop < chain:
            z_copies.append(
                send(dp_sum.at[step], z_got.at[step], (z_send, z_recv), step, z_id(hop))
            )

    all_copies, fwd_copies = [], []

    def stage_four(color):
        summed = dp_sum[color * chain + chain - 1].astype(F32)
        for hop in range(1, chain):
            z_copies[color * (chain - 1) + hop - 1].wait_recv()
            summed = summed + z_got[color * chain + hop - 1].astype(F32)
        final_ref[core, spot, :, lanes(color)] = summed.astype(BF16)
        mine = final_ref.at[core, spot, :, lanes(color)]
        for hop in range(1, chain):
            all_copies.append(
                send(mine, mine, (all_send, all_recv), color * chain + hop, z_id(hop))
            )
        fwd_copies.append(send(mine, mine, (fwd_send, fwd_recv), color * chain, partner))

    def stage_five(color):
        for hop in range(1, chain):
            all_copies[color * (chain - 1) + hop - 1].wait_recv()
            came = lax.rem(spot - hop + chain, chain)
            there = final_ref.at[core, came, :, lanes(color)]
            fwd_copies.append(send(there, there, (fwd_send, fwd_recv), color * chain + hop, partner))

    for color in range(COLORS):
        partials(core, keep_ref, color)
        for hop in range(chain):
            stage_one(color * chain + hop)

    grad_xn = nt(gproj[...], win_ref[...])
    grad_tokens = (grad + norm_back(grad_xn, normed, inverse)).astype(BF16)
    out_ref[...] = tn(fetch, grad_tokens).astype(BF16).reshape(packed)
    for step in range(COLORS * chain):
        stage_two(step)
        if step > 0:
            stage_three(step - 1)
        if step > chain and step % chain == 1:
            stage_four(step // chain - 1)
    ret_copies = [
        send(
            out_ref.at[dp_peer(step)],
            back_ref.at[me],
            (row_send, row_recv),
            3 * group + step,
            {"dp": dp_peer(step)},
        )
        for step in range(1, group)
    ]
    own = pltpu.make_async_copy(out_ref.at[me], back_ref.at[me], own_sems.at[3])
    own.start()
    stage_three(COLORS * chain - 1)
    stage_four(COLORS - 1)
    for color in range(COLORS - 1):
        stage_five(color)
    own.wait()
    for copy in ret_copies:
        copy.wait_recv()
    grad_ref[...] = tn(pick_ref[...], back_ref[...].reshape(total, width)).astype(BF16)
    stage_five(COLORS - 1)
    for copy in fwd_copies:
        copy.wait_recv()
    for copies in row_copies + (
        core_copies,
        one_copies,
        two_copies,
        z_copies,
        all_copies,
        fwd_copies,
        ret_copies,
    ):
        for copy in copies:
            copy.wait_send()


def finish_kernel(factor, grad_ref, final_ref, ev_ref, in_ref, out_ref):
    ev_ref[...] = grad_ref[...]
    share_in = in_ref.shape[0] // final_ref.shape[0]
    in_ref[...] = (final_ref[:, :share_in, :].astype(F32) * factor).reshape(in_ref.shape)
    out_ref[...] = (final_ref[:, share_in:, :].astype(F32) * factor).reshape(out_ref.shape)


def gather_kernel(pick_ref, back_ref, ev_ref):
    group, slots, width = back_ref.shape
    ev_ref[...] = tn(pick_ref[...], back_ref[...].reshape(group * slots, width)).astype(BF16)


VMEM = pl.BlockSpec(memory_space=pltpu.VMEM)
SMEM = pl.BlockSpec(memory_space=pltpu.SMEM)


def shape_of(shape, dtype=BF16):
    return jax.ShapeDtypeStruct(shape, dtype)


def swap(send, ident):
    group = send.shape[0]
    return pl.pallas_call(
        swap_kernel,
        out_shape=shape_of(send.shape),
        in_specs=[VMEM],
        out_specs=VMEM,
        scratch_shapes=[
            pltpu.SemaphoreType.DMA((group,)),
            pltpu.SemaphoreType.DMA((group,)),
            pltpu.SemaphoreType.DMA,
        ],
        compiler_params=pltpu.CompilerParams(collective_id=ident, has_side_effects=True),
        name="swap",
    )(send)


def body(events, cotangent, weight_in, weight_out, plan_dest, plan_pos, seq_lengths):
    group = lax.axis_size("dp")
    replicas = lax.axis_size("replica")
    rows, width = events.shape
    inner = weight_in.shape[1]
    slots = 3 * rows // (2 * group)
    total = group * slots
    chain = replicas // 2
    stacked = group == 4 and inner == group * width and width % (group * replicas * 16) == 0
    factor = 1.0 / (rows * group * replicas) ** 0.5
    outgoing_shape = shape_of((group, slots, width))
    wide = [
        pltpu.VMEM((rows, inner), BF16),
        pltpu.VMEM((rows, inner), F32),
    ]
    square = [
        pltpu.VMEM((HEADS, rows, rows), BF16),
        pltpu.VMEM((HEADS, rows, rows), F32),
    ]
    dest, place = plan_dest.reshape(1, rows), plan_pos.reshape(1, rows)
    if stacked:
        share_out = width // (group * replicas)
        depth = width // replicas + share_out
        piece = (depth, width)
        packed = pltpu.VMEM((group, slots, width), BF16)
        spots = pltpu.VMEM((group, 8, total), F32)
        halves = pltpu.VMEM((chain, group) + piece, BF16)
        count = COLORS * chain
        wave = (depth, width // COLORS)
        dma = pltpu.SemaphoreType.DMA
        grad_events, final = pl.pallas_call(
            functools.partial(whole_kernel, slots),
            out_shape=(shape_of((rows, width)), shape_of((2, chain) + piece)),
            in_specs=[SMEM] + [VMEM] * 4 + [pl.BlockSpec(memory_space=pl.ANY)] * 2,
            out_specs=(VMEM,) * 2,
            scratch_shapes=[
                pltpu.VMEM(weight_in.shape, BF16),
                pltpu.VMEM(weight_out.shape, BF16),
                pltpu.VMEM((total, rows), BF16),
                packed,
            ]
            + [packed, packed, spots] * 2
            + wide
            + [pltpu.VMEM((rows, inner), BF16)]
            + square
            + [
                pltpu.VMEM((rows, width), BF16),
                packed,
                pltpu.VMEM((2, chain, group, share_out, width), BF16),
                halves,
                halves,
                pltpu.VMEM((count, group) + wave, BF16),
                pltpu.VMEM((count, 2) + wave, BF16),
                pltpu.VMEM((count, 2) + wave, BF16),
                pltpu.VMEM((count, 2) + wave, F32),
                pltpu.VMEM((count,) + wave, BF16),
                pltpu.VMEM((count,) + wave, BF16),
                pltpu.VMEM((count,) + wave, BF16),
                pltpu.VMEM((count,) + wave, BF16),
                dma((4,)),
                dma,
                dma,
                dma((4 * group,)),
                dma((4 * group,)),
            ]
            + [dma((count,))] * 12,
            compiler_params=pltpu.CompilerParams(collective_id=0, has_side_effects=True),
            name="whole",
        )(seq_lengths, dest, place, events, cotangent, weight_in, weight_out)
        return pl.pallas_call(
            functools.partial(finish_kernel, factor),
            out_shape=(
                shape_of((rows, width)),
                shape_of((width, width), F32),
                shape_of((width // group, width), F32),
            ),
            grid=(2,),
            in_specs=[
                pl.BlockSpec((rows // 2, width), lambda i: (i, 0)),
                pl.BlockSpec((chain,) + piece, lambda i: (i, 0, 0)),
            ],
            out_specs=(
                pl.BlockSpec((rows // 2, width), lambda i: (i, 0)),
                pl.BlockSpec((width // 2, width), lambda i: (i, 0)),
                pl.BlockSpec((width // (2 * group), width), lambda i: (i, 0)),
            ),
            name="finish",
        )(grad_events, final.reshape((2 * chain,) + piece))
    send, pick = pl.pallas_call(
        functools.partial(prep_kernel, slots),
        out_shape=(shape_of((group, slots, 2 * width + LANES)), shape_of((total, rows))),
        in_specs=[VMEM] * 4,
        out_specs=(VMEM, VMEM),
        name="prep",
    )(dest, place, events, cotangent)
    recv = swap(send, 0)
    outgoing, normed_in, grad_proj, gated, grad_rows = pl.pallas_call(
        layer_kernel,
        out_shape=(
            outgoing_shape,
            shape_of((rows, width)),
            shape_of((rows, inner)),
            shape_of((rows, width)),
            shape_of((rows, width)),
        ),
        in_specs=[SMEM] + [VMEM] * 3,
        out_specs=(VMEM,) * 5,
        scratch_shapes=wide + square,
        name="layer",
    )(seq_lengths, recv, weight_in, weight_out)
    back = swap(outgoing, 1)
    grad_events = pl.pallas_call(
        gather_kernel,
        out_shape=shape_of((rows, width)),
        in_specs=[VMEM] * 2,
        out_specs=VMEM,
        name="finish",
    )(pick, back)
    rows_all = lax.all_gather(normed_in, "dp", axis=0, tiled=True)
    cot_all = lax.all_gather(grad_rows, "dp", axis=0, tiled=True)
    proj_cols = lax.all_to_all(grad_proj, "dp", split_axis=1, concat_axis=0, tiled=True)
    gated_cols = lax.all_to_all(gated, "dp", split_axis=1, concat_axis=0, tiled=True)
    shard_in = jnp.einsum("rd,rf->df", rows_all, proj_cols, preferred_element_type=F32)
    shard_out = jnp.einsum("re,rd->ed", gated_cols, cot_all, preferred_element_type=F32)
    total_in, total_out = lax.psum((shard_in, shard_out), "replica")
    return grad_events, total_in * factor, total_out * factor


def solution(mesh):
    return jax.shard_map(
        body,
        mesh=mesh,
        in_specs=(
            P(("dp", "replica"), None),
            P(("dp", "replica"), None),
            P(),
            P(),
            P(("dp", "replica")),
            P(("dp", "replica")),
            P(("dp", "replica"), None),
        ),
        out_specs=(P(("dp", "replica"), None), P(None, "dp"), P("dp", None)),
        check_vma=False,
    )
```

profile of v0, /device:TPU:0, one launch (start us, length us, event | category | flops | bytes accessed | tf_op | source)
XLA Modules:
  0.0 50.9 jit_solution(4822931451424955474)
XLA Ops:
  0.6 48.1 %whole.1 = (bf16[256,512]{1,0:T(8,128)(2,1)}, bf16[2,4,80,512]{3,2,1,0:T(8,128)(2,1)}) custom-call(s32[1,8]{1,0:T(1,128)} %len_ref.1, s32[1,256]{1,0:T(1,128)} %bitcast.4, s32[1,256]{1,0:T(1,128)} %bitcast.5, bf16[256,512]{1,0:T(8,128)(2,1)} %ev_ref.1, bf16[256,512]{1,0:T(8,128)(2,1)} %ct_ref.1, bf16[512,2048]{1,0:T(8,128)(2,1)} %win_any.1, ...), custom_call_target="tpu_custom_call" | custom-call | tf_op jit(solution)/shard_map/whole/pallas_call | solution.py:645
  48.7 2.2 %finish.1 = (bf16[256,512]{1,0:T(8,128)(2,1)}, f32[512,512]{1,0:T(8,128)}, f32[128,512]{1,0:T(8,128)}) custom-call(bf16[256,512]{1,0:T(8,128)(2,1)} %get-tuple-element.5.grad_ref, bf16[8,80,512]{2,1,0:T(8,128)(2,1)} %bitcast.3), custom_call_target="tpu_custom_call" | custom-call | tf_op jit(solution)/shard_map/finish/pallas_call | solution.py:684
where the time goes:
time: 51.4 us; the launch traced here: 50.9 us
  Pallas kernels  50.3 us (98%)
  between operations  0.64 us (1%)
    pallas_call x1, Pallas kernels, body(): pl.pallas_call(functools.partial(whole_kernel, slots), out_shape=(shape_o...  48.1 us
    pallas_call x1, Pallas kernels, body(): pl.pallas_call(functools.partial(finish_kernel, factor), out_shape=(shape...  2.24 us

commit v1 on v0

--- a/solution.py
+++ b/solution.py
@@ -200,6 +200,7 @@
 
 def whole_kernel(
     slots,
+    factor,
     len_ref,
     dest_ref,
     pos_ref,
@@ -208,6 +209,8 @@
     win_any,
     wout_any,
     grad_ref,
+    in_ref,
+    sum_ref,
     final_ref,
     win_ref,
     wout_ref,
@@ -562,6 +565,9 @@
     stage_five(COLORS - 1)
     for copy in fwd_copies:
         copy.wait_recv()
+    share = width // (2 * chain)
+    in_ref[...] = (final_ref[:, :, :share, :].astype(F32) * factor).reshape(in_ref.shape)
+    sum_ref[...] = (final_ref[:, :, share:, :].astype(F32) * factor).reshape(sum_ref.shape)
     for copies in row_copies + (
         core_copies,
         one_copies,
@@ -575,11 +581,16 @@
             copy.wait_send()
 
 
-def finish_kernel(factor, grad_ref, final_ref, ev_ref, in_ref, out_ref):
-    ev_ref[...] = grad_ref[...]
-    share_in = in_ref.shape[0] // final_ref.shape[0]
-    in_ref[...] = (final_ref[:, :share_in, :].astype(F32) * factor).reshape(in_ref.shape)
-    out_ref[...] = (final_ref[:, share_in:, :].astype(F32) * factor).reshape(out_ref.shape)
+def finish_kernel(*refs):
+    count = len(refs) // 2
+    sources, outs, sems = refs[:count], refs[count : 2 * count], refs[2 * count]
+    copies = [
+        pltpu.make_async_copy(sources[at], outs[at], sems.at[at]) for at in range(count)
+    ]
+    for copy in copies:
+        copy.start()
+    for copy in copies:
+        copy.wait()
 
 
 def gather_kernel(pick_ref, back_ref, ev_ref):
@@ -642,12 +653,17 @@
         count = COLORS * chain
         wave = (depth, width // COLORS)
         dma = pltpu.SemaphoreType.DMA
-        grad_events, final = pl.pallas_call(
-            functools.partial(whole_kernel, slots),
-            out_shape=(shape_of((rows, width)), shape_of((2, chain) + piece)),
+        results = pl.pallas_call(
+            functools.partial(whole_kernel, slots, factor),
+            out_shape=(
+                pltpu.VMEM((rows, width), BF16),
+                pltpu.VMEM((width, width), F32),
+                pltpu.VMEM((width // group, width), F32),
+            ),
             in_specs=[SMEM] + [VMEM] * 4 + [pl.BlockSpec(memory_space=pl.ANY)] * 2,
-            out_specs=(VMEM,) * 2,
+            out_specs=(VMEM,) * 3,
             scratch_shapes=[
+                pltpu.VMEM((2, chain) + piece, BF16),
                 pltpu.VMEM(weight_in.shape, BF16),
                 pltpu.VMEM(weight_out.shape, BF16),
                 pltpu.VMEM((total, rows), BF16),
@@ -682,24 +698,13 @@
             name="whole",
         )(seq_lengths, dest, place, events, cotangent, weight_in, weight_out)
         return pl.pallas_call(
-            functools.partial(finish_kernel, factor),
-            out_shape=(
-                shape_of((rows, width)),
-                shape_of((width, width), F32),
-                shape_of((width // group, width), F32),
-            ),
-            grid=(2,),
-            in_specs=[
-                pl.BlockSpec((rows // 2, width), lambda i: (i, 0)),
-                pl.BlockSpec((chain,) + piece, lambda i: (i, 0, 0)),
-            ],
-            out_specs=(
-                pl.BlockSpec((rows // 2, width), lambda i: (i, 0)),
-                pl.BlockSpec((width // 2, width), lambda i: (i, 0)),
-                pl.BlockSpec((width // (2 * group), width), lambda i: (i, 0)),
-            ),
+            finish_kernel,
+            out_shape=tuple(shape_of(value.shape, value.dtype) for value in results),
+            in_specs=[VMEM] * 3,
+            out_specs=(pl.BlockSpec(memory_space=pltpu.HBM),) * 3,
+            scratch_shapes=[pltpu.SemaphoreType.DMA((3,))],
             name="finish",
-        )(grad_events, final.reshape((2 * chain,) + piece))
+        )(*[pltpu.with_memory_space_constraint(value, pltpu.VMEM) for value in results])
     send, pick = pl.pallas_call(
         functools.partial(prep_kernel, slots),
         out_shape=(shape_of((group, slots, 2 * width + LANES)), shape_of((total, rows))),

time: 51.4 us -> 49.5 us (0.963)
  Pallas kernels: 50.3 us -> 48.3 us
    pallas_call x2, Pallas kernels: 50.3 us -> 48.3 us  [the longest x1 47.1 us: body(): pl.pallas_call(functools.partial(whole_kernel, slots, factor), out_shape=...]
where the time goes in v1:
time: 49.5 us; the launch traced here: 48.9 us
  Pallas kernels  48.3 us (98%)
  between operations  0.64 us (1%)
    pallas_call x1, Pallas kernels, body(): pl.pallas_call(functools.partial(whole_kernel, slots, factor), out_shape=...  47.1 us
    pallas_call x1, Pallas kernels, body(): pl.pallas_call(finish_kernel, out_shape=tuple((shape_of(value.shape, valu...  1.16 us

profile of v1, /device:TPU:0, one launch (start us, length us, event | category | flops | bytes accessed | tf_op | source)
XLA Modules:
  0.0 48.9 jit_solution(16386823875983469602)
XLA Ops:
  0.6 47.1 %whole.1 = (bf16[256,512]{1,0:T(8,128)(2,1)S(1)}, f32[512,512]{1,0:T(8,128)S(1)}, f32[128,512]{1,0:T(8,128)S(1)}) custom-call(s32[1,8]{1,0:T(1,128)} %len_ref.1, s32[1,256]{1,0:T(1,128)} %bitcast.2, s32[1,256]{1,0:T(1,128)} %bitcast.3, bf16[256,512]{1,0:T(8,128)(2,1)} %ev_ref.1, bf16[256,512]{1,0:T(8,128)(2,1)} %ct_ref.1, bf16[512,2048]{1,0:T(8,128)(2,1)} %win_any.1, ...), custom_call_target="tpu_custom_call" | custom-call | tf_op jit(solution)/shard_map/whole/pallas_call | solution.py:656
  47.8 1.2 %finish.1 = (bf16[256,512]{1,0:T(8,128)(2,1)}, f32[512,512]{1,0:T(8,128)}, f32[128,512]{1,0:T(8,128)}) custom-call(bf16[256,512]{1,0:T(8,128)(2,1)S(1)} %get-tuple-element.6.refs_0_, f32[512,512]{1,0:T(8,128)S(1)} %get-tuple-element.7.refs_1_, f32[128,512]{1,0:T(8,128)S(1)} %get-tuple-element.8.refs_2_), custom_call_target="tpu_custom_call" | custom-call | tf_op jit(solution)/shard_map/finish/pallas_call | solution.py:700

commit v2 on v1

--- a/solution.py
+++ b/solution.py
@@ -9,8 +9,8 @@
 
 HEADS = 8
 MAXLEN = 128
-COLORS = 1
 EPS = 1e-05
+RELAYED = 3
 LANES = 128
 MESH = pl.DeviceIdType.MESH
 F32 = jnp.float32
@@ -201,17 +201,22 @@
 def whole_kernel(
     slots,
     factor,
-    len_ref,
-    dest_ref,
-    pos_ref,
-    ev_ref,
-    ct_ref,
+    len_any,
+    dest_any,
+    pos_any,
+    ev_any,
+    ct_any,
     win_any,
     wout_any,
     grad_ref,
     in_ref,
     sum_ref,
     final_ref,
+    len_ref,
+    dest_ref,
+    pos_ref,
+    ev_ref,
+    ct_ref,
     win_ref,
     wout_ref,
     pick_ref,
@@ -229,38 +234,36 @@
     slope_s,
     xn_ref,
     out_ref,
-    b_ref,
-    give_ref,
-    keep_ref,
+    part_ref,
     core_got,
     one_send,
     one_got,
     two_keep,
     two_send,
     two_got,
-    dp_sum,
-    z_got,
-    own_sems,
-    win_sem,
-    wout_sem,
-    row_send,
-    row_recv,
-    core_send,
-    core_recv,
+    up_send,
+    rs_got,
+    load_sems,
+    row_ssem,
+    row_rsem,
+    core_ssem,
+    core_rsem,
     one_ssem,
     one_rsem,
     two_ssem,
     two_rsem,
-    z_send,
-    z_recv,
-    all_send,
-    all_recv,
-    fwd_send,
-    fwd_recv,
+    up_ssem,
+    up_rsem,
+    mid_rsem,
+    mate_ssem,
+    rim_ssem,
+    ag_rsem,
+    fwd_ssem,
+    fwd_rsem,
 ):
     rows, width = ev_ref.shape
     group = ev_send.shape[0]
-    chain = keep_ref.shape[0]
+    colors, depth, span = rs_got.shape[0], rs_got.shape[3], rs_got.shape[4]
     total = group * slots
     head = width // HEADS
     scale = 1.0 / head**0.5
@@ -273,40 +276,72 @@
     low_bit, high_bit = lax.rem(me, 2), me // 2
     near = high_bit * 2 + 1 - low_bit
     far = (1 - high_bit) * 2 + low_bit
-    first = other * near + core * far
-    second = core * near + other * far
     third = 3 - me
 
     def dp_peer(step):
         return lax.rem(me + step, group)
 
-    def z_peer(step):
-        return lax.rem(spot + step, chain)
-
-    def z_id(step):
-        return {"replica": z_peer(step) * 2 + core}
-
-    win_copy = pltpu.make_async_copy(win_any, win_ref, win_sem)
-    wout_copy = pltpu.make_async_copy(wout_any, wout_ref, wout_sem)
+    side = spot // 2
+    away = 1 - side
+    inner = (spot == 1) | (spot == 2)
+    outer = ~inner
+    hub = {"replica": (1 + side) * 2 + core}
+    mate = {"replica": (3 - spot) * 2 + core}
+    rim = {"replica": 3 * side * 2 + core}
+    far_hub = {"replica": (2 - side) * 2 + core}
+    far_rim = {"replica": 3 * away * 2 + core}
+
+    loads = [
+        pltpu.make_async_copy(source, target, load_sems.at[at])
+        for at, (source, target) in enumerate(
+            (
+                (ev_any, ev_ref),
+                (ct_any, ct_ref),
+                (win_any, win_ref),
+                (wout_any, wout_ref),
+                (dest_any, dest_ref),
+                (pos_any, pos_ref),
+                (len_any, len_ref),
+            )
+        )
+    ]
+    for at in (4, 0, 5, 1, 6):
+        loads[at].start()
     barrier = pltpu.get_barrier_semaphore()
     for step in range(1, group):
         pl.semaphore_signal(barrier, inc=1, device_id={"dp": dp_peer(step)}, device_id_type=MESH)
     pl.semaphore_signal(barrier, inc=1, device_id=partner, device_id_type=MESH)
-    for step in range(1, chain):
-        pl.semaphore_signal(barrier, inc=1, device_id=z_id(step), device_id_type=MESH)
-
-    def send(src, dst, sems, at, device):
-        copy = pltpu.make_async_remote_copy(
+
+    @pl.when(outer)
+    def _():
+        for device in (hub, far_hub):
+            pl.semaphore_signal(barrier, inc=1, device_id=device, device_id_type=MESH)
+
+    @pl.when(inner)
+    def _():
+        for device in (mate, rim, far_rim):
+            pl.semaphore_signal(barrier, inc=1, device_id=device, device_id_type=MESH)
+
+    def describe(src, dst, ssem, rsem, device):
+        return pltpu.make_async_remote_copy(
             src_ref=src,
             dst_ref=dst,
-            send_sem=sems[0].at[at],
-            recv_sem=sems[1].at[at],
+            send_sem=ssem,
+            recv_sem=rsem,
             device_id=device,
             device_id_type=MESH,
         )
-        copy.start()
-        return copy
-
+
+    def send(src, dst, ssem, rsem, device):
+        describe(src, dst, ssem, rsem, device).start()
+
+    def sent(like, ssem):
+        describe(like, like, ssem, ssem, partner).wait_send()
+
+    def came(like, rsem):
+        describe(like, like, rsem, rsem, partner).wait_recv()
+
+    loads[4].wait()
     dest = dest_ref[...]
     hot = lax.broadcasted_iota(jnp.int32, (8, rows), 0) == dest
     upper = lax.broadcasted_iota(jnp.int32, (rows, rows), 0) < lax.broadcasted_iota(
@@ -320,54 +355,49 @@
     pick = jnp.where(slot_iota == dest * slots + slot, 1.0, 0.0).astype(BF16)
     pick_ref[...] = pick
     packed = (group, slots, width)
+    loads[0].wait()
     ev_send[...] = nn(pick, ev_ref[...]).astype(BF16).reshape(packed)
-    win_copy.start()
-    wout_copy.start()
-    pl.semaphore_wait(barrier, group + chain - 1)
-    row_copies = ([], [], [])
-    own_copies = []
+    pl.semaphore_wait(barrier, group + 2 + jnp.where(inner, 1, 0))
 
     def rows_out(kind, src, dst):
-        for step in range(1, group):
-            peer = dp_peer(step)
-            row_copies[kind].append(
-                send(
-                    src.at[peer],
-                    dst.at[me],
-                    (row_send, row_recv),
-                    kind * group + step,
-                    {"dp": peer},
-                )
-            )
-        own = pltpu.make_async_copy(src.at[me], dst.at[me], own_sems.at[kind])
-        own.start()
-        own_copies.append(own)
-
-    rows_out(0, ev_send, ev_got)
+        for step in (3, 1, 2):
+            peer = step ^ me
+            send(src.at[peer], dst.at[me], row_ssem.at[kind], row_rsem.at[kind], {"dp": peer})
+        dst[me] = src[me]
+
+    def others(buffer):
+        return buffer.at[pl.ds(0, group - 1)]
+
+    rows_out(1, ev_send, ev_got)
+    loads[2].start()
+    loads[3].start()
+    loads[5].wait()
     spots = jnp.broadcast_to(pos_ref[...] + 1, (8, rows)).astype(F32).astype(BF16)
-    landing = slot_iota == me * slots + slot
+    lane_iota = lax.broadcasted_iota(jnp.int32, (LANES, rows), 0)
     for dp in range(group):
-        there = jnp.where(landing & (dest == dp), 1.0, 0.0).astype(BF16)
+        there = jnp.where((lane_iota == slot) & (dest == dp), 1.0, 0.0).astype(BF16)
         at_send[dp] = nt(spots, there)
-    rows_out(1, at_send, at_got)
+    rows_out(0, at_send, at_got)
+    loads[1].wait()
     ct_send[...] = nn(pick, ct_ref[...]).astype(BF16).reshape(packed)
+    sent(others(ev_send), row_ssem.at[1])
     rows_out(2, ct_send, ct_got)
 
-    for kind in range(2):
-        own_copies[kind].wait()
-        for copy in row_copies[kind]:
-            copy.wait_recv()
-    place = at_got[0]
-    for dp in range(1, group):
-        place = place + at_got[dp]
+    came(others(at_got), row_rsem.at[0])
+    came(others(ev_got), row_rsem.at[1])
+    place = jnp.zeros((8, total), F32)
+    blank = jnp.zeros((8, total - LANES), F32)
+    for dp in range(group):
+        there = jnp.concatenate([at_got[dp], blank], axis=1)
+        place = place + pltpu.roll(there, dp * slots, 1)
     row_iota = lax.broadcasted_iota(jnp.int32, (rows, total), 0).astype(F32) + 1.0
     fetch = jnp.where(row_iota == place[:1], 1.0, 0.0).astype(BF16)
     tokens = nn(fetch, ev_got[...].reshape(total, width))
     normed, inverse = normalize(tokens)
     xn = normed.astype(BF16)
     xn_ref[...] = xn
-    win_copy.wait()
-    wout_copy.wait()
+    loads[2].wait()
+    loads[3].wait()
     for block in range(4):
         cols = slice(block * width, (block + 1) * width)
         proj = nn(xn, win_ref[:, cols])
@@ -376,6 +406,7 @@
         slope_p[:, cols] = sig * (1.0 + proj * (1.0 - sig))
     row_at = lax.broadcasted_iota(jnp.int32, (rows, 1), 0)
     col_at = lax.broadcasted_iota(jnp.int32, (1, rows), 1)
+    loads[6].wait()
     bound = jnp.int32(0)
     row_seg = jnp.zeros((rows, 1), jnp.int32)
     col_seg = jnp.zeros((1, rows), jnp.int32)
@@ -413,20 +444,37 @@
     gate = act[:, :width].astype(F32)
     gated = (gate * onorm).astype(BF16)
 
-    own_copies[2].wait()
-    for copy in row_copies[2]:
-        copy.wait_recv()
+    came(others(ct_got), row_rsem.at[2])
     grad = nn(fetch, ct_got[...].reshape(total, width))
     grad16 = grad.astype(BF16)
+
+    def store_part(color, whole, row_of, column_of):
+        for edge in range(2):
+            for piece in range(4):
+                for dp in range(group):
+                    row, column = row_of(edge, piece, dp), column_of(edge, piece, dp)
+                    part_ref[color, edge, piece % 2, piece // 2, dp] = whole[
+                        row : row + depth, column : column + span
+                    ]
+        send(
+            part_ref.at[color, other],
+            core_got.at[color],
+            core_ssem.at[0],
+            core_rsem.at[color],
+            partner,
+        )
+
+    store_part(
+        0,
+        tn(gated, grad16).astype(BF16),
+        lambda edge, piece, dp: (2 * dp + edge) * depth,
+        lambda edge, piece, dp: piece * span,
+    )
     grad_z = nt(grad16, wout_ref[...])
     gproj[:, :width] = (grad_z * onorm * slope_p[:, :width]).astype(BF16)
-    share_in = width // (2 * chain)
-    share_out = width // (group * 2 * chain)
-    whole_out = tn(gated, grad16).astype(BF16).reshape(group, 2, chain, share_out, width)
-    for dp in range(group):
-        b_ref[:, :, dp] = whole_out[dp]
     grad_out = norm_back(grad_z * gate, onorm, oinv).astype(BF16)
-    for duo in range(HEADS // 2):
+
+    def back_duo(duo):
         value, query, key = cut(1, duo), cut(2, duo), cut(3, duo)
         gout = grad_out[:, duo * pair : (duo + 1) * pair]
         parts = ([], [], [])
@@ -442,143 +490,239 @@
             both = jnp.where(low, parts[block][0], parts[block][1])
             gproj[:, cols] = (both * slope_p[:, cols]).astype(BF16)
 
-    wave = width // COLORS
-
-    def lanes(color):
-        return slice(color * wave, (color + 1) * wave)
-
-    def partials(which, into, color):
-        across = width // 2
-        columns = pl.ds(pl.multiple_of(which * across, across), across)
-        left = xn_ref[:, columns]
-        for dp in range(group):
-            start = dp * width + color * wave
-            shard = tn(left, gproj[:, start : start + wave]).astype(BF16)
-            into[:, dp, :share_in, lanes(color)] = shard.reshape(chain, share_in, wave)
-        into[:, :, share_in:, lanes(color)] = b_ref[which, :, :, :, lanes(color)]
-
-    core_copies, one_copies, two_copies, z_copies = [], [], [], []
-    for color in range(COLORS):
-        partials(other, give_ref, color)
-        for hop in range(1, chain + 1):
-            step = color * chain + hop - 1
-            core_copies.append(
+    def stage_zero(duo):
+        columns = jnp.concatenate(
+            [
+                gproj[:, dp * width + duo * span : dp * width + (duo + 1) * span]
+                for dp in range(group)
+            ],
+            axis=1,
+        )
+        store_part(
+            duo + 1,
+            tn(xn_ref[...], columns).astype(BF16),
+            lambda edge, piece, dp: (4 * edge + piece) * depth,
+            lambda edge, piece, dp: dp * span,
+        )
+
+    def ways(way):
+        return (near, far) if way == 0 else (far, near)
+
+    def stage_one(color):
+        came(core_got.at[color], core_rsem.at[color])
+        for way in range(2):
+            first, second = ways(way)
+
+            def both(dp):
+                mine = part_ref[color, core, way, :, dp].astype(F32)
+                return mine + core_got[color, way, :, dp].astype(F32)
+
+            one_send[color, way, 0] = both(first).astype(BF16)
+            one_send[color, way, 1] = both(third).astype(BF16)
+            send(
+                one_send.at[color, way],
+                one_got.at[color, way],
+                one_ssem.at[0],
+                one_rsem.at[color],
+                {"dp": first},
+            )
+            two_keep[color, way, 0] = both(me)
+            two_keep[color, way, 1] = both(second)
+
+    def stage_two(color):
+        came(one_got.at[color], one_rsem.at[color])
+        for way in range(2):
+            two_send[color, way] = (
+                two_keep[color, way, 1] + one_got[color, way, 1].astype(F32)
+            ).astype(BF16)
+            send(
+                two_send.at[color, way],
+                two_got.at[color, way],
+                two_ssem.at[0],
+                two_rsem.at[color],
+                {"dp": ways(way)[1]},
+            )
+
+    def relayed(color):
+        return color < RELAYED
+
+    def stage_three(color):
+        came(two_got.at[color], two_rsem.at[color])
+        for way in range(2):
+            summed = (
+                two_keep[color, way, 0]
+                + one_got[color, way, 0].astype(F32)
+                + two_got[color, way].astype(F32)
+            )
+            two_keep[color, way, 0] = summed
+            up_send[color, :, way] = summed.astype(BF16)
+
+        @pl.when(outer)
+        def _():
+            if relayed(color):
+                target = rs_got.at[color, pl.ds(0, 2)]
+                send(up_send.at[color], target, up_ssem.at[0], up_rsem.at[color], hub)
+            else:
+                for slot, at, device in ((away, 2, far_hub), (side, 0, hub)):
+                    send(
+                        up_send.at[color, slot],
+                        rs_got.at[color, at],
+                        up_ssem.at[0],
+                        up_rsem.at[color],
+                        device,
+                    )
+
+        if not relayed(color):
+
+            @pl.when(inner)
+            def _():
                 send(
-                    give_ref.at[z_peer(hop), :, :, lanes(color)],
-                    core_got.at[step],
-                    (core_send, core_recv),
-                    step,
-                    partner,
+                    up_send.at[color, away],
+                    rs_got.at[color, 1],
+                    up_ssem.at[0],
+                    up_rsem.at[color],
+                    mate,
                 )
+
+    def stage_b(color):
+        @pl.when(inner)
+        def _():
+            came(rs_got.at[color, pl.ds(0, 2)], up_rsem.at[color])
+            for way in range(2):
+                up_send[color, away, way] = (
+                    two_keep[color, way, 0, away] + rs_got[color, away, way].astype(F32)
+                ).astype(BF16)
+            send(
+                up_send.at[color, away],
+                rs_got.at[color, 2],
+                up_ssem.at[0],
+                mid_rsem.at[color],
+                mate,
             )
 
-    def stage_one(step):
-        at = z_peer(step % chain + 1)
-        cols = lanes(step // chain)
-        core_copies[step].wait_recv()
-
-        def both(dp):
-            return keep_ref[at, dp, :, cols].astype(F32) + core_got[step, dp].astype(F32)
-
-        one_send[step, 0] = both(first).astype(BF16)
-        one_send[step, 1] = both(third).astype(BF16)
-        one_copies.append(
-            send(one_send.at[step], one_got.at[step], (one_ssem, one_rsem), step, {"dp": first})
-        )
-        two_keep[step, 0] = both(me)
-        two_keep[step, 1] = both(second)
-
-    def stage_two(step):
-        one_copies[step].wait_recv()
-        two_send[step] = (two_keep[step, 1] + one_got[step, 1].astype(F32)).astype(BF16)
-        two_copies.append(
-            send(two_send.at[step], two_got.at[step], (two_ssem, two_rsem), step, {"dp": second})
-        )
-
-    def stage_three(step):
-        two_copies[step].wait_recv()
-        dp_sum[step] = (
-            two_keep[step, 0] + one_got[step, 0].astype(F32) + two_got[step].astype(F32)
-        ).astype(BF16)
-        hop = step % chain + 1
-        if hop < chain:
-            z_copies.append(
-                send(dp_sum.at[step], z_got.at[step], (z_send, z_recv), step, z_id(hop))
-            )
-
-    all_copies, fwd_copies = [], []
-
-    def stage_four(color):
-        summed = dp_sum[color * chain + chain - 1].astype(F32)
-        for hop in range(1, chain):
-            z_copies[color * (chain - 1) + hop - 1].wait_recv()
-            summed = summed + z_got[color * chain + hop - 1].astype(F32)
-        final_ref[core, spot, :, lanes(color)] = summed.astype(BF16)
-        mine = final_ref.at[core, spot, :, lanes(color)]
-        for hop in range(1, chain):
-            all_copies.append(
-                send(mine, mine, (all_send, all_recv), color * chain + hop, z_id(hop))
-            )
-        fwd_copies.append(send(mine, mine, (fwd_send, fwd_recv), color * chain, partner))
-
-    def stage_five(color):
-        for hop in range(1, chain):
-            all_copies[color * (chain - 1) + hop - 1].wait_recv()
-            came = lax.rem(spot - hop + chain, chain)
-            there = final_ref.at[core, came, :, lanes(color)]
-            fwd_copies.append(send(there, there, (fwd_send, fwd_recv), color * chain + hop, partner))
-
-    for color in range(COLORS):
-        partials(core, keep_ref, color)
-        for hop in range(chain):
-            stage_one(color * chain + hop)
-
+    def stage_c(color):
+        @pl.when(inner)
+        def _():
+            if relayed(color):
+                came(rs_got.at[color, 2], mid_rsem.at[color])
+                terms = (side, 2)
+            else:
+                came(rs_got.at[color, pl.ds(0, 3)], up_rsem.at[color])
+                terms = (0, 1, 2)
+            for way in range(2):
+                summed = two_keep[color, way, 0, side]
+                for term in terms:
+                    summed = summed + rs_got[color, term, way].astype(F32)
+                final_ref[color, core, side, way] = summed.astype(BF16)
+            mine = final_ref.at[color, core, side]
+            if not relayed(color):
+                send(mine, mine, rim_ssem.at[0], ag_rsem.at[color], far_rim)
+            send(mine, mine, mate_ssem.at[0], ag_rsem.at[color], mate)
+            send(mine, mine, rim_ssem.at[0], ag_rsem.at[color], rim)
+            send(mine, mine, fwd_ssem.at[0], fwd_rsem.at[color], partner)
+
+    def stage_d(color):
+        @pl.when(inner)
+        def _():
+            there = final_ref.at[color, core, away]
+            came(there, ag_rsem.at[color])
+            if relayed(color):
+                send(there, there, rim_ssem.at[0], ag_rsem.at[color], rim)
+            send(there, there, fwd_ssem.at[0], fwd_rsem.at[color], partner)
+
+    def stage_e(color):
+        @pl.when(outer)
+        def _():
+            there = final_ref.at[color, core]
+            came(there, ag_rsem.at[color])
+            send(there, there, fwd_ssem.at[0], fwd_rsem.at[color], partner)
+
+    def stage_f(color):
+        came(final_ref.at[color, other], fwd_rsem.at[color])
+        if color == 0:
+            for edge in range(2):
+                for piece in range(4):
+                    rows_at = slice(edge * depth, (edge + 1) * depth)
+                    sum_ref[rows_at, piece * span : (piece + 1) * span] = (
+                        final_ref[0, edge, piece // 2, piece % 2].astype(F32) * factor
+                    )
+        else:
+            in_ref[:, (color - 1) * span : color * span] = (
+                final_ref[color].astype(F32) * factor
+            ).reshape(width, span)
+
+    back_duo(0)
+    stage_zero(0)
+    stage_one(0)
+    back_duo(1)
+    stage_zero(1)
+    stage_one(1)
+    back_duo(2)
+    stage_zero(2)
+    back_duo(3)
+    stage_zero(3)
+    stage_one(2)
+    stage_two(0)
+    stage_one(3)
     grad_xn = nt(gproj[...], win_ref[...])
+    stage_two(1)
+    stage_one(4)
+    stage_three(0)
     grad_tokens = (grad + norm_back(grad_xn, normed, inverse)).astype(BF16)
     out_ref[...] = tn(fetch, grad_tokens).astype(BF16).reshape(packed)
-    for step in range(COLORS * chain):
-        stage_two(step)
-        if step > 0:
-            stage_three(step - 1)
-        if step > chain and step % chain == 1:
-            stage_four(step // chain - 1)
-    ret_copies = [
-        send(
-            out_ref.at[dp_peer(step)],
-            back_ref.at[me],
-            (row_send, row_recv),
-            3 * group + step,
-            {"dp": dp_peer(step)},
-        )
-        for step in range(1, group)
-    ]
-    own = pltpu.make_async_copy(out_ref.at[me], back_ref.at[me], own_sems.at[3])
-    own.start()
-    stage_three(COLORS * chain - 1)
-    stage_four(COLORS - 1)
-    for color in range(COLORS - 1):
-        stage_five(color)
-    own.wait()
-    for copy in ret_copies:
-        copy.wait_recv()
+    stage_two(2)
+    stage_three(1)
+    stage_two(3)
+    stage_b(0)
+    stage_three(2)
+    stage_two(4)
+    stage_b(1)
+    stage_three(3)
+    stage_c(0)
+    stage_three(4)
+    rows_out(3, out_ref, back_ref)
+    stage_b(2)
+    stage_c(1)
+    stage_d(0)
+    stage_c(2)
+    stage_c(3)
+    stage_d(1)
+    stage_e(0)
+    stage_c(4)
+    stage_d(2)
+    stage_d(3)
+    stage_e(1)
+    stage_e(2)
+    stage_d(4)
+    came(others(back_ref), row_rsem.at[3])
     grad_ref[...] = tn(pick_ref[...], back_ref[...].reshape(total, width)).astype(BF16)
-    stage_five(COLORS - 1)
-    for copy in fwd_copies:
-        copy.wait_recv()
-    share = width // (2 * chain)
-    in_ref[...] = (final_ref[:, :, :share, :].astype(F32) * factor).reshape(in_ref.shape)
-    sum_ref[...] = (final_ref[:, :, share:, :].astype(F32) * factor).reshape(sum_ref.shape)
-    for copies in row_copies + (
-        core_copies,
-        one_copies,
-        two_copies,
-        z_copies,
-        all_copies,
-        fwd_copies,
-        ret_copies,
-    ):
-        for copy in copies:
-            copy.wait_send()
+    stage_f(0)
+    stage_e(3)
+    stage_f(1)
+    stage_f(2)
+    stage_e(4)
+    stage_f(3)
+    stage_f(4)
+    sent(others(at_send), row_ssem.at[0])
+    sent(others(ct_send), row_ssem.at[2])
+    sent(others(out_ref), row_ssem.at[3])
+    sent(core_got, core_ssem.at[0])
+    sent(one_send, one_ssem.at[0])
+    sent(two_send, two_ssem.at[0])
+    half_of = final_ref.at[pl.ds(0, colors), 0, 0]
+    whole_of = final_ref.at[pl.ds(0, colors), 0]
+
+    @pl.when(inner)
+    def _():
+        sent(half_of, up_ssem.at[0])
+        sent(half_of, mate_ssem.at[0])
+        sent(whole_of, rim_ssem.at[0])
+
+    @pl.when(outer)
+    def _():
+        sent(whole_of, up_ssem.at[0])
+
+    sent(whole_of, fwd_ssem.at[0])
 
 
 def finish_kernel(*refs):
@@ -631,7 +775,18 @@
     slots = 3 * rows // (2 * group)
     total = group * slots
     chain = replicas // 2
-    stacked = group == 4 and inner == group * width and width % (group * replicas * 16) == 0
+    pair = 2 * width // HEADS
+    depth = width // (2 * chain)
+    stacked = (
+        group == 4
+        and chain == 4
+        and inner == group * width
+        and pair * chain == width
+        and pair % LANES == 0
+        and depth % 16 == 0
+        and slots <= LANES
+        and total % LANES == 0
+    )
     factor = 1.0 / (rows * group * replicas) ** 0.5
     outgoing_shape = shape_of((group, slots, width))
     wide = [
@@ -644,14 +799,12 @@
     ]
     dest, place = plan_dest.reshape(1, rows), plan_pos.reshape(1, rows)
     if stacked:
-        share_out = width // (group * replicas)
-        depth = width // replicas + share_out
-        piece = (depth, width)
         packed = pltpu.VMEM((group, slots, width), BF16)
-        spots = pltpu.VMEM((group, 8, total), F32)
-        halves = pltpu.VMEM((chain, group) + piece, BF16)
-        count = COLORS * chain
-        wave = (depth, width // COLORS)
+        spots = pltpu.VMEM((group, 8, LANES), F32)
+        duos = HEADS // 2
+        colors = duos + 1
+        piece = (depth, pair)
+        sized = lambda *lead, dtype=BF16: pltpu.VMEM(lead + piece, dtype)
         dma = pltpu.SemaphoreType.DMA
         results = pl.pallas_call(
             functools.partial(whole_kernel, slots, factor),
@@ -660,10 +813,15 @@
                 pltpu.VMEM((width, width), F32),
                 pltpu.VMEM((width // group, width), F32),
             ),
-            in_specs=[SMEM] + [VMEM] * 4 + [pl.BlockSpec(memory_space=pl.ANY)] * 2,
+            in_specs=[pl.BlockSpec(memory_space=pl.ANY)] * 7,
             out_specs=(VMEM,) * 3,
             scratch_shapes=[
-                pltpu.VMEM((2, chain) + piece, BF16),
+                sized(colors, 2, 2, 2),
+                pltpu.SMEM(seq_lengths.shape, jnp.int32),
+                pltpu.VMEM((1, rows), jnp.int32),
+                pltpu.VMEM((1, rows), jnp.int32),
+                pltpu.VMEM((rows, width), BF16),
+                pltpu.VMEM((rows, width), BF16),
                 pltpu.VMEM(weight_in.shape, BF16),
                 pltpu.VMEM(weight_out.shape, BF16),
                 pltpu.VMEM((total, rows), BF16),
@@ -676,24 +834,22 @@
             + [
                 pltpu.VMEM((rows, width), BF16),
                 packed,
-                pltpu.VMEM((2, chain, group, share_out, width), BF16),
-                halves,
-                halves,
-                pltpu.VMEM((count, group) + wave, BF16),
-                pltpu.VMEM((count, 2) + wave, BF16),
-                pltpu.VMEM((count, 2) + wave, BF16),
-                pltpu.VMEM((count, 2) + wave, F32),
-                pltpu.VMEM((count,) + wave, BF16),
-                pltpu.VMEM((count,) + wave, BF16),
-                pltpu.VMEM((count,) + wave, BF16),
-                pltpu.VMEM((count,) + wave, BF16),
+                sized(colors, 2, 2, 2, group),
+                sized(colors, 2, 2, group),
+                sized(colors, 2, 2, 2),
+                sized(colors, 2, 2, 2),
+                sized(colors, 2, 2, 2, dtype=F32),
+                sized(colors, 2, 2),
+                sized(colors, 2, 2),
+                sized(colors, 2, 2),
+                sized(colors, 3, 2),
+                dma((7,)),
                 dma((4,)),
-                dma,
-                dma,
-                dma((4 * group,)),
-                dma((4 * group,)),
+                dma((4,)),
             ]
-            + [dma((count,))] * 12,
+            + [dma((1,)), dma((colors,))] * 3
+            + [dma((1,)), dma((colors,)), dma((RELAYED,)), dma((1,)), dma((1,)), dma((colors,))]
+            + [dma((1,)), dma((colors,))],
             compiler_params=pltpu.CompilerParams(collective_id=0, has_side_effects=True),
             name="whole",
         )(seq_lengths, dest, place, events, cotangent, weight_in, weight_out)

time: 49.5 us -> 47.6 us (0.962)
  Pallas kernels: 48.3 us -> 46.8 us
    pallas_call x1, Pallas kernels: 47.1 us -> 45.6 us  [body(): pl.pallas_call(functools.partial(whole_kernel, slots, factor), out_shape=...]
where the time goes in v2:
time: 47.6 us; the launch traced here: 47.4 us
  Pallas kernels  46.8 us (98%)
  between operations  0.64 us (1%)
    pallas_call x1, Pallas kernels, body(): pl.pallas_call(functools.partial(whole_kernel, slots, factor), out_shape=...  45.6 us
    pallas_call x1, Pallas kernels, body(): pl.pallas_call(finish_kernel, out_shape=tuple((shape_of(value.shape, valu...  1.16 us

profile of v2, /device:TPU:0, one launch (start us, length us, event | category | flops | bytes accessed | tf_op | source)
XLA Modules:
  0.0 47.4 jit_solution(9133272691760241422)
XLA Ops:
  0.6 45.6 %whole.1 = (bf16[256,512]{1,0:T(8,128)(2,1)S(1)}, f32[512,512]{1,0:T(8,128)S(1)}, f32[128,512]{1,0:T(8,128)S(1)}) custom-call(s32[1,8]{1,0:T(1,128)} %len_any.1, s32[1,256]{1,0:T(1,128)} %bitcast.2, s32[1,256]{1,0:T(1,128)} %bitcast.3, bf16[256,512]{1,0:T(8,128)(2,1)} %ev_any.1, bf16[256,512]{1,0:T(8,128)(2,1)} %ct_any.1, bf16[512,2048]{1,0:T(8,128)(2,1)} %win_any.1, ...), custom_call_target="tpu_custom_call" | custom-call | tf_op jit(solution)/shard_map/whole/pallas_call | solution.py:809
  46.3 1.2 %finish.1 = (bf16[256,512]{1,0:T(8,128)(2,1)}, f32[512,512]{1,0:T(8,128)}, f32[128,512]{1,0:T(8,128)}) custom-call(bf16[256,512]{1,0:T(8,128)(2,1)S(1)} %get-tuple-element.6.refs_0_, f32[512,512]{1,0:T(8,128)S(1)} %get-tuple-element.7.refs_1_, f32[128,512]{1,0:T(8,128)S(1)} %get-tuple-element.8.refs_2_), custom_call_target="tpu_custom_call" | custom-call | tf_op jit(solution)/shard_map/finish/pallas_call | solution.py:856

commit v3 on v2

--- a/solution.py
+++ b/solution.py
@@ -10,7 +10,8 @@
 HEADS = 8
 MAXLEN = 128
 EPS = 1e-05
-RELAYED = 3
+RELAYED = 0
+ECHOED = 2
 LANES = 128
 MESH = pl.DeviceIdType.MESH
 F32 = jnp.float32
@@ -546,6 +547,9 @@
     def relayed(color):
         return color < RELAYED
 
+    def echoed(color):
+        return color < ECHOED
+
     def stage_three(color):
         came(two_got.at[color], two_rsem.at[color])
         for way in range(2):
@@ -585,6 +589,9 @@
                 )
 
     def stage_b(color):
+        if not relayed(color):
+            return
+
         @pl.when(inner)
         def _():
             came(rs_got.at[color, pl.ds(0, 2)], up_rsem.at[color])
@@ -615,7 +622,7 @@
                     summed = summed + rs_got[color, term, way].astype(F32)
                 final_ref[color, core, side, way] = summed.astype(BF16)
             mine = final_ref.at[color, core, side]
-            if not relayed(color):
+            if not echoed(color):
                 send(mine, mine, rim_ssem.at[0], ag_rsem.at[color], far_rim)
             send(mine, mine, mate_ssem.at[0], ag_rsem.at[color], mate)
             send(mine, mine, rim_ssem.at[0], ag_rsem.at[color], rim)
@@ -626,7 +633,7 @@
         def _():
             there = final_ref.at[color, core, away]
             came(there, ag_rsem.at[color])
-            if relayed(color):
+            if echoed(color):
                 send(there, there, rim_ssem.at[0], ag_rsem.at[color], rim)
             send(there, there, fwd_ssem.at[0], fwd_rsem.at[color], partner)
 
@@ -652,8 +659,8 @@
             ).reshape(width, span)
 
     back_duo(0)
+    stage_one(0)
     stage_zero(0)
-    stage_one(0)
     back_duo(1)
     stage_zero(1)
     stage_one(1)
@@ -661,48 +668,44 @@
     stage_zero(2)
     back_duo(3)
     stage_zero(3)
+    stage_two(0)
     stage_one(2)
-    stage_two(0)
-    stage_one(3)
     grad_xn = nt(gproj[...], win_ref[...])
     stage_two(1)
+    stage_one(3)
     stage_one(4)
-    stage_three(0)
     grad_tokens = (grad + norm_back(grad_xn, normed, inverse)).astype(BF16)
     out_ref[...] = tn(fetch, grad_tokens).astype(BF16).reshape(packed)
+    stage_three(0)
     stage_two(2)
     stage_three(1)
     stage_two(3)
-    stage_b(0)
+    stage_two(4)
     stage_three(2)
-    stage_two(4)
     stage_b(1)
+    stage_c(0)
     stage_three(3)
-    stage_c(0)
     stage_three(4)
     rows_out(3, out_ref, back_ref)
+    stage_c(1)
     stage_b(2)
-    stage_c(1)
+    stage_c(2)
     stage_d(0)
-    stage_c(2)
+    stage_e(0)
     stage_c(3)
     stage_d(1)
-    stage_e(0)
+    stage_e(1)
     stage_c(4)
     stage_d(2)
+    stage_e(2)
     stage_d(3)
-    stage_e(1)
-    stage_e(2)
+    stage_e(3)
     stage_d(4)
     came(others(back_ref), row_rsem.at[3])
     grad_ref[...] = tn(pick_ref[...], back_ref[...].reshape(total, width)).astype(BF16)
-    stage_f(0)
-    stage_e(3)
-    stage_f(1)
-    stage_f(2)
     stage_e(4)
-    stage_f(3)
-    stage_f(4)
+    for color in range(colors):
+        stage_f(color)
     sent(others(at_send), row_ssem.at[0])
     sent(others(ct_send), row_ssem.at[2])
     sent(others(out_ref), row_ssem.at[3])
@@ -848,7 +851,7 @@
                 dma((4,)),
             ]
             + [dma((1,)), dma((colors,))] * 3
-            + [dma((1,)), dma((colors,)), dma((RELAYED,)), dma((1,)), dma((1,)), dma((colors,))]
+            + [dma((1,)), dma((colors,)), dma((max(RELAYED, 1),)), dma((1,)), dma((1,)), dma((colors,))]
             + [dma((1,)), dma((colors,))],
             compiler_params=pltpu.CompilerParams(collective_id=0, has_side_effects=True),
             name="whole",

time: 47.6 us -> 44.4 us (0.933)
  Pallas kernels: 46.8 us -> 43.6 us
    pallas_call x1, Pallas kernels: 45.6 us -> 42.4 us  [body(): pl.pallas_call(functools.partial(whole_kernel, slots, factor), out_shape=...]
where the time goes in v3:
time: 44.4 us; the launch traced here: 44.2 us
  Pallas kernels  43.6 us (98%)
  between operations  0.64 us (1%)
    pallas_call x1, Pallas kernels, body(): pl.pallas_call(functools.partial(whole_kernel, slots, factor), out_shape=...  42.4 us
    pallas_call x1, Pallas kernels, body(): pl.pallas_call(finish_kernel, out_shape=tuple((shape_of(value.shape, valu...  1.16 us

profile of v3, /device:TPU:0, one launch (start us, length us, event | category | flops | bytes accessed | tf_op | source)
XLA Modules:
  0.0 44.2 jit_solution(3637880534900028267)
XLA Ops:
  0.6 42.4 %whole.1 = (bf16[256,512]{1,0:T(8,128)(2,1)S(1)}, f32[512,512]{1,0:T(8,128)S(1)}, f32[128,512]{1,0:T(8,128)S(1)}) custom-call(s32[1,8]{1,0:T(1,128)} %len_any.1, s32[1,256]{1,0:T(1,128)} %bitcast.2, s32[1,256]{1,0:T(1,128)} %bitcast.3, bf16[256,512]{1,0:T(8,128)(2,1)} %ev_any.1, bf16[256,512]{1,0:T(8,128)(2,1)} %ct_any.1, bf16[512,2048]{1,0:T(8,128)(2,1)} %win_any.1, ...), custom_call_target="tpu_custom_call" | custom-call | tf_op jit(solution)/shard_map/whole/pallas_call | solution.py:812
  43.0 1.2 %finish.1 = (bf16[256,512]{1,0:T(8,128)(2,1)}, f32[512,512]{1,0:T(8,128)}, f32[128,512]{1,0:T(8,128)}) custom-call(bf16[256,512]{1,0:T(8,128)(2,1)S(1)} %get-tuple-element.6.refs_0_, f32[512,512]{1,0:T(8,128)S(1)} %get-tuple-element.7.refs_1_, f32[128,512]{1,0:T(8,128)S(1)} %get-tuple-element.8.refs_2_), custom_call_target="tpu_custom_call" | custom-call | tf_op jit(solution)/shard_map/finish/pallas_call | solution.py:859

commit v4 on v3

--- a/solution.py
+++ b/solution.py
@@ -10,8 +10,8 @@
 HEADS = 8
 MAXLEN = 128
 EPS = 1e-05
-RELAYED = 0
 ECHOED = 2
+PAIRED = 2
 LANES = 128
 MESH = pl.DeviceIdType.MESH
 F32 = jnp.float32
@@ -244,6 +244,9 @@
     two_got,
     up_send,
     rs_got,
+    pair_send,
+    pair_keep,
+    pair_got,
     load_sems,
     row_ssem,
     row_rsem,
@@ -255,7 +258,9 @@
     two_rsem,
     up_ssem,
     up_rsem,
-    mid_rsem,
+    pair_ssem,
+    pair_rsem,
+    cross_ssem,
     mate_ssem,
     rim_ssem,
     ag_rsem,
@@ -289,6 +294,9 @@
     hub = {"replica": (1 + side) * 2 + core}
     mate = {"replica": (3 - spot) * 2 + core}
     rim = {"replica": 3 * side * 2 + core}
+    keep = 1 - lax.rem((spot + 1) // 2, 2)
+    give = 1 - keep
+    pal = {"replica": (spot + 1 - 2 * lax.rem(spot, 2)) * 2 + core}
     far_hub = {"replica": (2 - side) * 2 + core}
     far_rim = {"replica": 3 * away * 2 + core}
 
@@ -315,7 +323,7 @@
 
     @pl.when(outer)
     def _():
-        for device in (hub, far_hub):
+        for device in (hub, far_hub, far_rim):
             pl.semaphore_signal(barrier, inc=1, device_id=device, device_id_type=MESH)
 
     @pl.when(inner)
@@ -358,7 +366,7 @@
     packed = (group, slots, width)
     loads[0].wait()
     ev_send[...] = nn(pick, ev_ref[...]).astype(BF16).reshape(packed)
-    pl.semaphore_wait(barrier, group + 2 + jnp.where(inner, 1, 0))
+    pl.semaphore_wait(barrier, group + 3)
 
     def rows_out(kind, src, dst):
         for step in (3, 1, 2):
@@ -544,9 +552,6 @@
                 {"dp": ways(way)[1]},
             )
 
-    def relayed(color):
-        return color < RELAYED
-
     def echoed(color):
         return color < ECHOED
 
@@ -563,62 +568,32 @@
 
         @pl.when(outer)
         def _():
-            if relayed(color):
-                target = rs_got.at[color, pl.ds(0, 2)]
-                send(up_send.at[color], target, up_ssem.at[0], up_rsem.at[color], hub)
-            else:
-                for slot, at, device in ((away, 2, far_hub), (side, 0, hub)):
-                    send(
-                        up_send.at[color, slot],
-                        rs_got.at[color, at],
-                        up_ssem.at[0],
-                        up_rsem.at[color],
-                        device,
-                    )
-
-        if not relayed(color):
-
-            @pl.when(inner)
-            def _():
+            for slot, at, device in ((away, 2, far_hub), (side, 0, hub)):
                 send(
-                    up_send.at[color, away],
-                    rs_got.at[color, 1],
+                    up_send.at[color, slot],
+                    rs_got.at[color, at],
                     up_ssem.at[0],
                     up_rsem.at[color],
-                    mate,
+                    device,
                 )
-
-    def stage_b(color):
-        if not relayed(color):
-            return
 
         @pl.when(inner)
         def _():
-            came(rs_got.at[color, pl.ds(0, 2)], up_rsem.at[color])
-            for way in range(2):
-                up_send[color, away, way] = (
-                    two_keep[color, way, 0, away] + rs_got[color, away, way].astype(F32)
-                ).astype(BF16)
             send(
                 up_send.at[color, away],
-                rs_got.at[color, 2],
+                rs_got.at[color, 1],
                 up_ssem.at[0],
-                mid_rsem.at[color],
+                up_rsem.at[color],
                 mate,
             )
 
     def stage_c(color):
         @pl.when(inner)
         def _():
-            if relayed(color):
-                came(rs_got.at[color, 2], mid_rsem.at[color])
-                terms = (side, 2)
-            else:
-                came(rs_got.at[color, pl.ds(0, 3)], up_rsem.at[color])
-                terms = (0, 1, 2)
+            came(rs_got.at[color], up_rsem.at[color])
             for way in range(2):
                 summed = two_keep[color, way, 0, side]
-                for term in terms:
+                for term in range(3):
                     summed = summed + rs_got[color, term, way].astype(F32)
                 final_ref[color, core, side, way] = summed.astype(BF16)
             mine = final_ref.at[color, core, side]
@@ -643,6 +618,80 @@
             there = final_ref.at[color, core]
             came(there, ag_rsem.at[color])
             send(there, there, fwd_ssem.at[0], fwd_rsem.at[color], partner)
+
+    def pair_zero(color):
+        came(core_got.at[color], core_rsem.at[color])
+        for way in range(2):
+            for dp in range(group):
+
+                def both(slot):
+                    mine = part_ref[color, core, way, slot, dp].astype(F32)
+                    return mine + core_got[color, way, slot, dp].astype(F32)
+
+                pair_send[way, dp] = both(give).astype(BF16)
+                pair_keep[way, dp] = both(keep)
+        send(pair_send, pair_got, pair_ssem.at[0], pair_rsem.at[0], pal)
+
+    def pair_one(color):
+        came(pair_got, pair_rsem.at[0])
+        for way in range(2):
+            first, second = ways(way)
+
+            def both(dp):
+                return pair_keep[way, dp] + pair_got[way, dp].astype(F32)
+
+            one_send[color, way, 0, 0] = both(first).astype(BF16)
+            one_send[color, way, 0, 1] = both(third).astype(BF16)
+            send(
+                one_send.at[color, way, 0],
+                one_got.at[color, way, 0],
+                one_ssem.at[1],
+                one_rsem.at[color],
+                {"dp": first},
+            )
+            two_keep[color, way, 0, 0] = both(me)
+            two_keep[color, way, 0, 1] = both(second)
+
+    def pair_two(color):
+        came(one_got.at[color, pl.ds(0, 2), 0], one_rsem.at[color])
+        for way in range(2):
+            two_send[color, way, 0] = (
+                two_keep[color, way, 0, 1] + one_got[color, way, 0, 1].astype(F32)
+            ).astype(BF16)
+            send(
+                two_send.at[color, way, 0],
+                two_got.at[color, way, 0],
+                two_ssem.at[1],
+                two_rsem.at[color],
+                {"dp": ways(way)[1]},
+            )
+
+    def pair_three(color):
+        came(two_got.at[color, pl.ds(0, 2), 0], two_rsem.at[color])
+        for way in range(2):
+            up_send[color, 0, way] = (
+                two_keep[color, way, 0, 0]
+                + one_got[color, way, 0, 0].astype(F32)
+                + two_got[color, way, 0].astype(F32)
+            ).astype(BF16)
+        send(
+            up_send.at[color, 0], rs_got.at[color, 0], cross_ssem.at[0], up_rsem.at[color], mate
+        )
+
+    def pair_four(color):
+        came(rs_got.at[color, 0], up_rsem.at[color])
+        for way in range(2):
+            final_ref[color, core, keep, way] = (
+                up_send[color, 0, way].astype(F32) + rs_got[color, 0, way].astype(F32)
+            ).astype(BF16)
+        mine = final_ref.at[color, core, keep]
+        send(mine, mine, cross_ssem.at[0], ag_rsem.at[color], pal)
+        send(mine, mine, fwd_ssem.at[0], fwd_rsem.at[color], partner)
+
+    def pair_five(color):
+        there = final_ref.at[color, core, give]
+        came(there, ag_rsem.at[color])
+        send(there, there, fwd_ssem.at[0], fwd_rsem.at[color], partner)
 
     def stage_f(color):
         came(final_ref.at[color, other], fwd_rsem.at[color])
@@ -659,48 +708,46 @@
             ).reshape(width, span)
 
     back_duo(0)
+    stage_zero(0)
     stage_one(0)
-    stage_zero(0)
     back_duo(1)
     stage_zero(1)
     stage_one(1)
     back_duo(2)
     stage_zero(2)
+    pair_zero(PAIRED)
     back_duo(3)
     stage_zero(3)
     stage_two(0)
-    stage_one(2)
+    stage_one(3)
     grad_xn = nt(gproj[...], win_ref[...])
     stage_two(1)
-    stage_one(3)
     stage_one(4)
     grad_tokens = (grad + norm_back(grad_xn, normed, inverse)).astype(BF16)
     out_ref[...] = tn(fetch, grad_tokens).astype(BF16).reshape(packed)
     stage_three(0)
-    stage_two(2)
+    pair_one(PAIRED)
+    stage_two(3)
     stage_three(1)
-    stage_two(3)
     stage_two(4)
-    stage_three(2)
-    stage_b(1)
+    pair_two(PAIRED)
+    stage_three(3)
     stage_c(0)
-    stage_three(3)
     stage_three(4)
+    pair_three(PAIRED)
     rows_out(3, out_ref, back_ref)
     stage_c(1)
-    stage_b(2)
-    stage_c(2)
+    stage_c(3)
     stage_d(0)
+    stage_c(4)
+    pair_four(PAIRED)
+    stage_d(1)
     stage_e(0)
-    stage_c(3)
-    stage_d(1)
+    pair_five(PAIRED)
+    stage_d(3)
     stage_e(1)
-    stage_c(4)
-    stage_d(2)
-    stage_e(2)
-    stage_d(3)
+    stage_d(4)
     stage_e(3)
-    stage_d(4)
     came(others(back_ref), row_rsem.at[3])
     grad_ref[...] = tn(pick_ref[...], back_ref[...].reshape(total, width)).astype(BF16)
     stage_e(4)
@@ -710,10 +757,15 @@
     sent(others(ct_send), row_ssem.at[2])
     sent(others(out_ref), row_ssem.at[3])
     sent(core_got, core_ssem.at[0])
-    sent(one_send, one_ssem.at[0])
-    sent(two_send, two_ssem.at[0])
-    half_of = final_ref.at[pl.ds(0, colors), 0, 0]
-    whole_of = final_ref.at[pl.ds(0, colors), 0]
+    plain = pl.ds(0, colors - 1)
+    sent(one_send.at[plain], one_ssem.at[0])
+    sent(two_send.at[plain], two_ssem.at[0])
+    sent(final_ref.at[0, 0], one_ssem.at[1])
+    sent(final_ref.at[0, 0, 0], two_ssem.at[1])
+    sent(pair_send, pair_ssem.at[0])
+    sent(final_ref.at[0, 0], cross_ssem.at[0])
+    half_of = final_ref.at[plain, 0, 0]
+    whole_of = final_ref.at[plain, 0]
 
     @pl.when(inner)
     def _():
@@ -725,7 +777,7 @@
     def _():
         sent(whole_of, up_ssem.at[0])
 
-    sent(whole_of, fwd_ssem.at[0])
+    sent(final_ref.at[pl.ds(0, colors), 0], fwd_ssem.at[0])
 
 
 def finish_kernel(*refs):
@@ -846,13 +898,18 @@
                 sized(colors, 2, 2),
                 sized(colors, 2, 2),
                 sized(colors, 3, 2),
+                sized(2, group),
+                sized(2, group, dtype=F32),
+                sized(2, group),
                 dma((7,)),
                 dma((4,)),
                 dma((4,)),
             ]
-            + [dma((1,)), dma((colors,))] * 3
-            + [dma((1,)), dma((colors,)), dma((max(RELAYED, 1),)), dma((1,)), dma((1,)), dma((colors,))]
-            + [dma((1,)), dma((colors,))],
+            + [dma((1,)), dma((colors,))]
+            + [dma((2,)), dma((colors,))] * 2
+            + [dma((1,)), dma((colors,))]
+            + [dma((1,))] * 5
+            + [dma((colors,)), dma((1,)), dma((colors,))],
             compiler_params=pltpu.CompilerParams(collective_id=0, has_side_effects=True),
             name="whole",
         )(seq_lengths, dest, place, events, cotangent, weight_in, weight_out)

time: 44.4 us -> 43.2 us (0.973)
  Pallas kernels: 43.6 us -> 42.4 us
    pallas_call x1, Pallas kernels: 42.4 us -> 41.3 us  [body(): pl.pallas_call(functools.partial(whole_kernel, slots, factor), out_shape=...]
where the time goes in v4:
time: 43.2 us; the launch traced here: 43.1 us
  Pallas kernels  42.4 us (98%)
  between operations  0.64 us (1%)
    pallas_call x1, Pallas kernels, body(): pl.pallas_call(functools.partial(whole_kernel, slots, factor), out_shape=...  41.3 us
    pallas_call x1, Pallas kernels, body(): pl.pallas_call(finish_kernel, out_shape=tuple((shape_of(value.shape, valu...  1.16 us

profile of v4, /device:TPU:0, one launch (start us, length us, event | category | flops | bytes accessed | tf_op | source)
XLA Modules:
  0.0 43.1 jit_solution(12778137055176787538)
XLA Ops:
  0.6 41.3 %whole.1 = (bf16[256,512]{1,0:T(8,128)(2,1)S(1)}, f32[512,512]{1,0:T(8,128)S(1)}, f32[128,512]{1,0:T(8,128)S(1)}) custom-call(s32[1,8]{1,0:T(1,128)} %len_any.1, s32[1,256]{1,0:T(1,128)} %bitcast.2, s32[1,256]{1,0:T(1,128)} %bitcast.3, bf16[256,512]{1,0:T(8,128)(2,1)} %ev_any.1, bf16[256,512]{1,0:T(8,128)(2,1)} %ct_any.1, bf16[512,2048]{1,0:T(8,128)(2,1)} %win_any.1, ...), custom_call_target="tpu_custom_call" | custom-call | tf_op jit(solution)/shard_map/whole/pallas_call | solution.py:864
  41.9 1.2 %finish.1 = (bf16[256,512]{1,0:T(8,128)(2,1)}, f32[512,512]{1,0:T(8,128)}, f32[128,512]{1,0:T(8,128)}) custom-call(bf16[256,512]{1,0:T(8,128)(2,1)S(1)} %get-tuple-element.6.refs_0_, f32[512,512]{1,0:T(8,128)S(1)} %get-tuple-element.7.refs_1_, f32[128,512]{1,0:T(8,128)S(1)} %get-tuple-element.8.refs_2_), custom_call_target="tpu_custom_call" | custom-call | tf_op jit(solution)/shard_map/finish/pallas_call | solution.py:916

commit v5 on v4

--- a/solution.py
+++ b/solution.py
@@ -248,6 +248,7 @@
     pair_keep,
     pair_got,
     load_sems,
+    turn_sem,
     row_ssem,
     row_rsem,
     core_ssem,
@@ -389,8 +390,19 @@
     rows_out(0, at_send, at_got)
     loads[1].wait()
     ct_send[...] = nn(pick, ct_ref[...]).astype(BF16).reshape(packed)
-    sent(others(ev_send), row_ssem.at[1])
-    rows_out(2, ct_send, ct_got)
+
+    @pl.when(core == 0)
+    def _():
+        rows_out(2, ct_send, ct_got)
+        sent(others(ev_send), row_ssem.at[1])
+        pl.semaphore_signal(turn_sem, inc=1, device_id=partner, device_id_type=MESH)
+
+    @pl.when(core == 1)
+    def _():
+        sent(others(ev_send), row_ssem.at[1])
+        pl.semaphore_wait(turn_sem, 1)
+        rows_out(2, ct_send, ct_got)
+
 
     came(others(at_got), row_rsem.at[0])
     came(others(ev_got), row_rsem.at[1])
@@ -743,13 +755,13 @@
     pair_four(PAIRED)
     stage_d(1)
     stage_e(0)
+    came(others(back_ref), row_rsem.at[3])
+    grad_ref[...] = tn(pick_ref[...], back_ref[...].reshape(total, width)).astype(BF16)
     pair_five(PAIRED)
     stage_d(3)
     stage_e(1)
     stage_d(4)
     stage_e(3)
-    came(others(back_ref), row_rsem.at[3])
-    grad_ref[...] = tn(pick_ref[...], back_ref[...].reshape(total, width)).astype(BF16)
     stage_e(4)
     for color in range(colors):
         stage_f(color)
@@ -902,6 +914,7 @@
                 sized(2, group, dtype=F32),
                 sized(2, group),
                 dma((7,)),
+                pltpu.SemaphoreType.REGULAR,
                 dma((4,)),
                 dma((4,)),
             ]

time: 43.2 us -> 42.7 us (0.988)
  Pallas kernels: 42.4 us -> 41.9 us
    pallas_call x1, Pallas kernels: 41.3 us -> 40.8 us  [body(): pl.pallas_call(functools.partial(whole_kernel, slots, factor), out_shape=...]
where the time goes in v5:
time: 42.7 us; the launch traced here: 42.6 us
  Pallas kernels  41.9 us (98%)
  between operations  0.64 us (1%)
    pallas_call x1, Pallas kernels, body(): pl.pallas_call(functools.partial(whole_kernel, slots, factor), out_shape=...  40.8 us
    pallas_call x1, Pallas kernels, body(): pl.pallas_call(finish_kernel, out_shape=tuple((shape_of(value.shape, valu...  1.16 us

profile of v5, /device:TPU:0, one launch (start us, length us, event | category | flops | bytes accessed | tf_op | source)
XLA Modules:
  0.0 42.6 jit_solution(13080761732007886672)
XLA Ops:
  0.6 40.8 %whole.1 = (bf16[256,512]{1,0:T(8,128)(2,1)S(1)}, f32[512,512]{1,0:T(8,128)S(1)}, f32[128,512]{1,0:T(8,128)S(1)}) custom-call(s32[1,8]{1,0:T(1,128)} %len_any.1, s32[1,256]{1,0:T(1,128)} %bitcast.2, s32[1,256]{1,0:T(1,128)} %bitcast.3, bf16[256,512]{1,0:T(8,128)(2,1)} %ev_any.1, bf16[256,512]{1,0:T(8,128)(2,1)} %ct_any.1, bf16[512,2048]{1,0:T(8,128)(2,1)} %win_any.1, ...), custom_call_target="tpu_custom_call" | custom-call | tf_op jit(solution)/shard_map/whole/pallas_call | solution.py:876
  41.4 1.2 %finish.1 = (bf16[256,512]{1,0:T(8,128)(2,1)}, f32[512,512]{1,0:T(8,128)}, f32[128,512]{1,0:T(8,128)}) custom-call(bf16[256,512]{1,0:T(8,128)(2,1)S(1)} %get-tuple-element.6.refs_0_, f32[512,512]{1,0:T(8,128)S(1)} %get-tuple-element.7.refs_1_, f32[128,512]{1,0:T(8,128)S(1)} %get-tuple-element.8.refs_2_), custom_call_target="tpu_custom_call" | custom-call | tf_op jit(solution)/shard_map/finish/pallas_call | solution.py:929

commit v6 on v5

--- a/solution.py
+++ b/solution.py
@@ -10,7 +10,7 @@
 HEADS = 8
 MAXLEN = 128
 EPS = 1e-05
-ECHOED = 2
+ECHOED = 1
 PAIRED = 2
 LANES = 128
 MESH = pl.DeviceIdType.MESH
@@ -367,27 +367,27 @@
     packed = (group, slots, width)
     loads[0].wait()
     ev_send[...] = nn(pick, ev_ref[...]).astype(BF16).reshape(packed)
-    pl.semaphore_wait(barrier, group + 3)
-
-    def rows_out(kind, src, dst):
-        for step in (3, 1, 2):
-            peer = step ^ me
-            send(src.at[peer], dst.at[me], row_ssem.at[kind], row_rsem.at[kind], {"dp": peer})
-        dst[me] = src[me]
-
-    def others(buffer):
-        return buffer.at[pl.ds(0, group - 1)]
-
-    rows_out(1, ev_send, ev_got)
-    loads[2].start()
-    loads[3].start()
     loads[5].wait()
     spots = jnp.broadcast_to(pos_ref[...] + 1, (8, rows)).astype(F32).astype(BF16)
     lane_iota = lax.broadcasted_iota(jnp.int32, (LANES, rows), 0)
     for dp in range(group):
         there = jnp.where((lane_iota == slot) & (dest == dp), 1.0, 0.0).astype(BF16)
         at_send[dp] = nt(spots, there)
+    pl.semaphore_wait(barrier, group + 3)
+
+    def rows_out(kind, src, dst):
+        for step in (3, 1, 2):
+            peer = step ^ me
+            send(src.at[peer], dst.at[me], row_ssem.at[kind], row_rsem.at[kind], {"dp": peer})
+        dst[me] = src[me]
+
+    def others(buffer):
+        return buffer.at[pl.ds(0, group - 1)]
+
     rows_out(0, at_send, at_got)
+    rows_out(1, ev_send, ev_got)
+    loads[2].start()
+    loads[3].start()
     loads[1].wait()
     ct_send[...] = nn(pick, ct_ref[...]).astype(BF16).reshape(packed)
 
@@ -405,7 +405,6 @@
 
 
     came(others(at_got), row_rsem.at[0])
-    came(others(ev_got), row_rsem.at[1])
     place = jnp.zeros((8, total), F32)
     blank = jnp.zeros((8, total - LANES), F32)
     for dp in range(group):
@@ -413,6 +412,17 @@
         place = place + pltpu.roll(there, dp * slots, 1)
     row_iota = lax.broadcasted_iota(jnp.int32, (rows, total), 0).astype(F32) + 1.0
     fetch = jnp.where(row_iota == place[:1], 1.0, 0.0).astype(BF16)
+    row_at = lax.broadcasted_iota(jnp.int32, (rows, 1), 0)
+    col_at = lax.broadcasted_iota(jnp.int32, (1, rows), 1)
+    loads[6].wait()
+    bound = jnp.int32(0)
+    row_seg = jnp.zeros((rows, 1), jnp.int32)
+    col_seg = jnp.zeros((1, rows), jnp.int32)
+    for seq in range(len_ref.shape[1]):
+        bound = bound + len_ref[0, seq]
+        row_seg = row_seg + jnp.where(row_at >= bound, 1, 0)
+        col_seg = col_seg + jnp.where(col_at >= bound, 1, 0)
+    came(others(ev_got), row_rsem.at[1])
     tokens = nn(fetch, ev_got[...].reshape(total, width))
     normed, inverse = normalize(tokens)
     xn = normed.astype(BF16)
@@ -425,16 +435,6 @@
         sig = jax.nn.sigmoid(proj)
         act[:, cols] = (proj * sig).astype(BF16)
         slope_p[:, cols] = sig * (1.0 + proj * (1.0 - sig))
-    row_at = lax.broadcasted_iota(jnp.int32, (rows, 1), 0)
-    col_at = lax.broadcasted_iota(jnp.int32, (1, rows), 1)
-    loads[6].wait()
-    bound = jnp.int32(0)
-    row_seg = jnp.zeros((rows, 1), jnp.int32)
-    col_seg = jnp.zeros((1, rows), jnp.int32)
-    for seq in range(len_ref.shape[1]):
-        bound = bound + len_ref[0, seq]
-        row_seg = row_seg + jnp.where(row_at >= bound, 1, 0)
-        col_seg = col_seg + jnp.where(col_at >= bound, 1, 0)
     mask = (row_seg == col_seg) & (col_at <= row_at)
     pair = 2 * head
     low = lax.broadcasted_iota(jnp.int32, (rows, pair), 1) < head
@@ -464,10 +464,10 @@
     onorm, oinv = normalize(jnp.concatenate(outs, axis=1))
     gate = act[:, :width].astype(F32)
     gated = (gate * onorm).astype(BF16)
+    gated_slots = tn(fetch, gated).astype(BF16)
 
     came(others(ct_got), row_rsem.at[2])
-    grad = nn(fetch, ct_got[...].reshape(total, width))
-    grad16 = grad.astype(BF16)
+    ct_slots = ct_got[...].reshape(total, width)
 
     def store_part(color, whole, row_of, column_of):
         for edge in range(2):
@@ -487,11 +487,12 @@
 
     store_part(
         0,
-        tn(gated, grad16).astype(BF16),
+        tn(gated_slots, ct_slots).astype(BF16),
         lambda edge, piece, dp: (2 * dp + edge) * depth,
         lambda edge, piece, dp: piece * span,
     )
-    grad_z = nt(grad16, wout_ref[...])
+    grad = nn(fetch, ct_slots)
+    grad_z = nt(grad.astype(BF16), wout_ref[...])
     gproj[:, :width] = (grad_z * onorm * slope_p[:, :width]).astype(BF16)
     grad_out = norm_back(grad_z * gate, onorm, oinv).astype(BF16)
 
@@ -720,8 +721,8 @@
             ).reshape(width, span)
 
     back_duo(0)
+    stage_one(0)
     stage_zero(0)
-    stage_one(0)
     back_duo(1)
     stage_zero(1)
     stage_one(1)

time: 42.7 us -> 42.5 us (level)
  no operation moved by 1% of the time
where the time goes in v6:
time: 42.5 us; the launch traced here: 42.3 us
  Pallas kernels  41.7 us (98%)
  between operations  0.64 us (2%)
    pallas_call x1, Pallas kernels, body(): pl.pallas_call(functools.partial(whole_kernel, slots, factor), out_shape=...  40.5 us
    pallas_call x1, Pallas kernels, body(): pl.pallas_call(finish_kernel, out_shape=tuple((shape_of(value.shape, valu...  1.16 us

profile of v6, /device:TPU:0, one launch (start us, length us, event | category | flops | bytes accessed | tf_op | source)
XLA Modules:
  0.0 42.3 jit_solution(14146587404779886386)
XLA Ops:
  0.6 40.5 %whole.1 = (bf16[256,512]{1,0:T(8,128)(2,1)S(1)}, f32[512,512]{1,0:T(8,128)S(1)}, f32[128,512]{1,0:T(8,128)S(1)}) custom-call(s32[1,8]{1,0:T(1,128)} %len_any.1, s32[1,256]{1,0:T(1,128)} %bitcast.2, s32[1,256]{1,0:T(1,128)} %bitcast.3, bf16[256,512]{1,0:T(8,128)(2,1)} %ev_any.1, bf16[256,512]{1,0:T(8,128)(2,1)} %ct_any.1, bf16[512,2048]{1,0:T(8,128)(2,1)} %win_any.1, ...), custom_call_target="tpu_custom_call" | custom-call | tf_op jit(solution)/shard_map/whole/pallas_call | solution.py:877
  41.2 1.2 %finish.1 = (bf16[256,512]{1,0:T(8,128)(2,1)}, f32[512,512]{1,0:T(8,128)}, f32[128,512]{1,0:T(8,128)}) custom-call(bf16[256,512]{1,0:T(8,128)(2,1)S(1)} %get-tuple-element.6.refs_0_, f32[512,512]{1,0:T(8,128)S(1)} %get-tuple-element.7.refs_1_, f32[128,512]{1,0:T(8,128)S(1)} %get-tuple-element.8.refs_2_), custom_call_target="tpu_custom_call" | custom-call | tf_op jit(solution)/shard_map/finish/pallas_call | solution.py:930
